TPU v7x, 32 devices: a whole 2x2x4 slice. The times are simulated.
32 devices in a mesh: blk: 4 (over y, x), grp: 8 (over z, core).
Axes of the slice: x: 2, y: 2, z: 4, core: 2. Of those that a mesh axis runs over, the one named last changes fastest.
Arguments:
- frames: bfloat16 [4096, 8, 2048], P(('blk', 'grp')), may hold values from -6 to 6
- counts: int32 [4096], P(('blk', 'grp')), may hold values from 1 to 8
- positives: int32 [4096], P(('blk', 'grp')), may hold values from 0 to 4095, as said below
- w_first: bfloat16 [2048, 4096], P(None, 'grp'), may hold values from -0.125 to 0.125
- w_second: bfloat16 [4096, 256], P('grp'), may hold values from -0.09375 to 0.09375
Outputs:
- batch_loss: float32 [], replicated
- grad_first: float32 [2048, 4096], P(None, 'grp')
- grad_second: float32 [4096, 256], P('grp')
Inputs may be any that keep to these rules, and one draw needn't show every extreme that they name: positives[positives[i]] = i and positives[i] != i for every clip i.
All inputs are finite; a program needn't handle non-finite values.
Results may differ from a plain program's by a relative error of at most 0.005.
The roundings to bfloat16 on the way count: a program that leaves them out, or rounds other values in their place, can miss the bound.
Values may be sent and summed in bfloat16 or wider, within the bound.
A program may use at most 128 MiB of HBM per device.

v0:
```python
import jax
import jax.numpy as jnp
from jax import lax
from jax.sharding import PartitionSpec as P

logit_sharpness_divisor = 0.05
score_top = 20.0


def shifted(block, axis, distance):
    devices = range(lax.axis_size(axis))
    route = [((i - distance) % len(devices), i) for i in devices]
    return lax.ppermute(block, axis, route)


def shards(frames, counts, positives, w_first, w_second):
    row_count = frames.shape[0]
    slot_count = frames.shape[1]
    cycle_size = lax.axis_size("blk")
    group_size = lax.axis_size("grp")
    complete_segment_entries = row_count * cycle_size * group_size
    group_rows = row_count * group_size
    cycle_index = lax.axis_index("blk")
    first_row = (cycle_index * group_size + lax.axis_index("grp")) * row_count
    row_ids = first_row + jnp.arange(row_count, dtype=jnp.int32)
    frame_mask = (jnp.arange(slot_count, dtype=jnp.int32)[None, :] < counts[:, None]).astype(
        jnp.bfloat16
    )
    summed = jnp.einsum("rf,rfc->rc", frame_mask, frames, preferred_element_type=jnp.float32)
    pooled = (summed / counts[:, None].astype(jnp.float32)).astype(jnp.bfloat16)
    pooled_all = lax.all_gather(pooled, "grp", axis=0, tiled=True)
    preact = jnp.dot(pooled_all, w_first, preferred_element_type=jnp.float32)
    hidden = jax.nn.gelu(preact).astype(jnp.bfloat16)
    raw_keys = lax.psum_scatter(
        jnp.dot(hidden, w_second, preferred_element_type=jnp.float32),
        "grp",
        scatter_dimension=0,
        tiled=True,
    )
    key_length = jnp.sqrt(jnp.sum(raw_keys * raw_keys, axis=1, keepdims=True) + 1e-06)
    unit_keys = raw_keys / key_length
    lower_match_vectors = unit_keys.astype(jnp.bfloat16)
    key_block = lax.all_gather(lower_match_vectors, "grp", axis=0, tiled=True)
    block_ids = jnp.arange(group_rows, dtype=jnp.int32)
    exp_total = jnp.zeros((row_count,), jnp.float32)
    pos_score = jnp.zeros((row_count,), jnp.float32)
    stored = []
    for hop_index in range(cycle_size):
        owner = (cycle_index - hop_index) % cycle_size
        offset = owner * group_rows
        key_ids = offset + block_ids
        cosine_logit_matrix = (
            lax.dot_general(
                lower_match_vectors,
                key_block,
                (((1,), (1,)), ((), ())),
                preferred_element_type=jnp.float32,
            )
            / logit_sharpness_divisor
        )
        self_mask = key_ids[None, :] == row_ids[:, None]
        pair_mask = key_ids[None, :] == positives[:, None]
        exp_total = exp_total + jnp.sum(
            jnp.where(self_mask, 0.0, jnp.exp(cosine_logit_matrix - score_top)), axis=1
        )
        pos_score = pos_score + jnp.sum(jnp.where(pair_mask, cosine_logit_matrix, 0.0), axis=1)
        stored.append((key_block, offset, cosine_logit_matrix, self_mask, pair_mask))
        if hop_index + 1 < cycle_size:
            key_block = shifted(key_block, "blk", 1)
    log_norm = jnp.log(exp_total) + score_top
    batch_loss = lax.psum(jnp.sum(log_norm - pos_score), ("blk", "grp")) / complete_segment_entries
    query_gradient = jnp.zeros((row_count, lower_match_vectors.shape[1]), jnp.float32)
    every_norm = lax.all_gather(log_norm, ("blk", "grp"), axis=0, tiled=True)
    self_key_gradient = jnp.zeros((row_count, lower_match_vectors.shape[1]), jnp.float32)
    for key_block, offset, cosine_logit_matrix, self_mask, pair_mask in stored:
        pair_float = pair_mask.astype(jnp.float32)
        probs = jnp.where(self_mask, 0.0, jnp.exp(cosine_logit_matrix - log_norm[:, None]))
        weights = (probs - pair_float).astype(jnp.bfloat16)
        column_norm = lax.dynamic_slice_in_dim(every_norm, offset, group_rows, 0)
        mirrored = jnp.where(self_mask, 0.0, jnp.exp(cosine_logit_matrix - column_norm[None, :]))
        mirror_weights = (mirrored - pair_float).astype(jnp.bfloat16)
        query_gradient = query_gradient + jnp.dot(
            weights, key_block, preferred_element_type=jnp.float32
        )
        self_key_gradient = self_key_gradient + jnp.dot(
            mirror_weights, key_block, preferred_element_type=jnp.float32
        )
    sphere_projected_derivative = (query_gradient + self_key_gradient) / (
        complete_segment_entries * logit_sharpness_divisor
    )
    raw_grad = (
        (
            sphere_projected_derivative
            - unit_keys * jnp.sum(unit_keys * sphere_projected_derivative, axis=1, keepdims=True)
        )
        / key_length
    ).astype(jnp.bfloat16)
    group_grad = lax.all_gather(raw_grad, "grp", axis=0, tiled=True)
    second_grad = lax.dot_general(
        hidden, group_grad, (((0,), (0,)), ((), ())), preferred_element_type=jnp.float32
    )
    hidden_grad = lax.dot_general(
        group_grad, w_second, (((1,), (1,)), ((), ())), preferred_element_type=jnp.float32
    )
    unused, backward = jax.vjp(jax.nn.gelu, preact)
    preact_grad = backward(hidden_grad)[0].astype(jnp.bfloat16)
    first_grad = lax.dot_general(
        pooled_all, preact_grad, (((0,), (0,)), ((), ())), preferred_element_type=jnp.float32
    )
    first_grad, second_grad = lax.psum((first_grad, second_grad), "blk")
    return (batch_loss, first_grad, second_grad)


def solution(mesh):
    return jax.shard_map(
        shards,
        mesh=mesh,
        in_specs=(
            P(("blk", "grp"), None, None),
            P(("blk", "grp")),
            P(("blk", "grp")),
            P(None, "grp"),
            P("grp", None),
        ),
        out_specs=(P(), P(None, "grp"), P("grp", None)),
        check_vma=False,
    )
```

profile of v0, /device:TPU:0, one launch (start us, length us, event | category | flops | bytes accessed | tf_op | source)
XLA Modules:
  0.0 355.8 jit_solution(10595022451589504186)
XLA Ops:
  7.2 0.0 copy-start
  7.2 0.0 all-gather.3.cloned.1.call-start
  7.2 0.9 fusion.81
  8.1 0.7 convert_element_type.56
  8.8 3.4 fusion.63
  12.2 1.2 fusion.9
  13.4 0.0 all-gather.3.cloned.1.call-update
  13.4 0.0 copy-start.5
  13.4 0.0 reduce-scatter.2.cloned.1.call-start
  13.4 49.7 %all-gather.3.cloned.1.call-done = bf16[1024,2048]{1,0:T(8,128)(2,1)} async-done(((bf16[128,2048]{1,0:T(8,128)(2,1)}), bf16[1024,2048]{1,0:T(8,128)(2,1)}) %all-gather.3.cloned.1.call-update) | async-done | bytes 4194320 | tf_op jit(solution)/shard_map/all_gather | solution.py:31
  63.1 6.2 %multiply_convert_fusion = (bf16[1024,512]{1,0:T(8,128)(2,1)S(1)}, f32[1024,512]{1,0:T(8,128)}) fusion(bf16[1024,2048]{1,0:T(8,128)(2,1)} %all-gather.3.cloned.1.call-done, bf16[2048,512]{1,0:T(8,128)(2,1)S(1)} %copy-done), kind=kOutput, calls=%fused_computation.9 | convolution fusion | flops 2152202240 | bytes 9437184 | tf_op jit(solution)/shard_map/dot_general | solution.py:32
  69.3 1.0 copy-done.2
  70.3 1.4 fusion.98
  71.7 0.0 reduce-scatter.2.cloned.1.call-update
  71.7 0.0 all-reduce.3.cloned.1.call-start
  71.8 31.5 %reduce-scatter.2.cloned.1.call-done = f32[128,256]{1,0:T(8,128)} async-done(((f32[1024,256]{1,0:T(8,128)}), f32[128,256]{1,0:T(8,128)}) %reduce-scatter.2.cloned.1.call-update) | async-done | bytes 131088 | tf_op jit(solution)/shard_map/reduce_scatter | solution.py:34
  103.3 1.0 multiply_reduce_fusion.1
  104.3 1.0 fusion.96
  105.3 0.0 copy-start.6
  105.3 14.9 %all_gather.13 = bf16[1024,256]{1,0:T(8,128)(2,1)S(1)} all-gather(bf16[128,256]{1,0:T(8,128)(2,1)S(1)} %fusion.96), channel_id=1, replica_groups=mesh['blk'=4,'grp'=8] {'grp'}, dimensions={0}, use_global_device_ids=true | all-gather | bytes 589824 | tf_op jit(solution)/shard_map/all_gather | solution.py:43
  120.3 1.4 collective-permute-start
  121.7 13.6 %collective-permute-done = bf16[1024,256]{1,0:T(8,128)(2,1)S(1)} collective-permute-done((bf16[1024,256]{1,0:T(8,128)(2,1)S(1)}, bf16[1024,256]{1,0:T(8,128)(2,1)S(1)}, u32[]{:S(2)}, u32[]{:S(2)}) %collective-permute-start) | collective-permute-done | bytes 524320 | tf_op jit(solution)/shard_map/ppermute | solution.py:13
  135.4 0.5 collective-permute-start.1
  135.9 13.8 %collective-permute-done.1 = bf16[1024,256]{1,0:T(8,128)(2,1)} collective-permute-done((bf16[1024,256]{1,0:T(8,128)(2,1)S(1)}, bf16[1024,256]{1,0:T(8,128)(2,1)}, u32[]{:S(2)}, u32[]{:S(2)}) %collective-permute-start.1) | collective-permute-done | bytes 524320 | tf_op jit(solution)/shard_map/ppermute | solution.py:13
  149.7 0.3 convolution_multiply_fusion.3
  150.0 0.3 convolution_multiply_fusion.2
  150.3 1.3 convolution_multiply_fusion.1
  151.7 11.6 %collective-permute-done.2 = bf16[1024,256]{1,0:T(8,128)(2,1)S(1)} collective-permute-done((bf16[1024,256]{1,0:T(8,128)(2,1)}, bf16[1024,256]{1,0:T(8,128)(2,1)S(1)}, u32[]{:S(2)}, u32[]{:S(2)}) %collective-permute-start.2) | collective-permute-done | bytes 524320 | tf_op jit(solution)/shard_map/ppermute | solution.py:13
  163.3 0.9 fusion.22
  164.1 0.6 subtract_reduce_fusion
  164.7 0.3 fusion.37
  165.1 36.9 %all-gather = f32[32,1,128]{2,1,0:T(1,128)S(1)} all-gather(f32[1,1,128]{2,1,0:T(1,128)S(1)} %bitcast.35), channel_id=1, replica_groups=mesh['blk'=4,'grp'=8] {'blk','grp'}, dimensions={0}, use_global_device_ids=true | all-gather | bytes 16896 | tf_op jit(solution)/shard_map/all_gather | solution.py:73
  201.9 0.3 fusion.35
  202.3 0.3 convolution_add_fusion.5
  202.6 1.4 convolution_add_fusion.4
  204.0 0.3 convolution_add_fusion.2
  204.3 1.4 convolution_add_fusion.1
  205.7 0.3 convolution_add_fusion
  206.1 0.4 multiply_reduce_fusion
  206.5 0.1 divide_convert_fusion
  206.6 14.9 %all_gather.15 = bf16[1024,256]{1,0:T(8,128)(2,1)S(1)} all-gather(bf16[128,256]{1,0:T(8,128)(2,1)S(1)} %divide_convert_fusion), channel_id=1, replica_groups=mesh['blk'=4,'grp'=8] {'grp'}, dimensions={0}, use_global_device_ids=true | all-gather | bytes 589824 | tf_op jit(solution)/shard_map/all_gather | solution.py:98
  221.6 1.3 fusion.99
  222.8 8.5 %fusion.10 = f32[2048,512]{1,0:T(8,128)} fusion(bf16[1024,2048]{1,0:T(8,128)(2,1)} %all-gather.3.cloned.1.call-done, f32[1024,512]{1,0:T(8,128)} %get-tuple-element.26, bf16[1024,256]{1,0:T(8,128)(2,1)S(1)} %all_gather.15, bf16[512,256]{1,0:T(8,128)(2,1)S(1)} %copy-done.5), kind=kOutput, calls=%fused_computation.24 | convolution fusion | flops 2426404864 | bytes 11272192 | tf_op jit(solution)/shard_map/dot_general | solution.py:107
  231.3 0.0 all-reduce.3.cloned.1.call-update
  231.3 38.3 %psum.21 = f32[]{:T(128)} all-reduce(f32[]{:T(128)} %get-tuple-element.19), channel_id=1, replica_groups=mesh['blk'=4,'grp'=8] {'blk','grp'}, use_global_device_ids=true, to_apply=%region_11.12 | all-reduce | flops 1 | bytes 8 | tf_op jit(solution)/shard_map/psum | solution.py:71
  270.3 72.4 %all-reduce.3.cloned.1.call-done = (f32[2048,512]{1,0:T(8,128)}, f32[512,256]{1,0:T(8,128)}) async-done(((f32[2048,512]{1,0:T(8,128)}, f32[512,256]{1,0:T(8,128)}), (f32[2048,512]{1,0:T(8,128)}, f32[512,256]{1,0:T(8,128)})) %all-reduce.3.cloned.1.call-update) | async-done | bytes 4718608 | tf_op jit(solution)/shard_map/psum | solution.py:110
  342.7 4.7 %copy.16 = f32[2048,512]{1,0:T(8,128)} copy(f32[2048,512]{1,0:T(8,128)} %get-tuple-element.35) | data formatting | bytes 8388608
  347.4 0.8 copy.17
  (16 shorter events, 0.0 us)
Async XLA Ops:
  7.2 56.0 %copy-start = (bf16[2048,512]{1,0:T(8,128)(2,1)S(1)}, bf16[2048,512]{1,0:T(8,128)(2,1)}, u32[]{:S(2)}) copy-start(bf16[2048,512]{1,0:T(8,128)(2,1)} %param.8) | copy-start | bytes 6291460
  7.2 55.9 %all-gather.3.cloned.1.call-start = ((), (), s32[]{:S(2)}) async-start(), calls=%async_computation.1 | async-start | bytes 4718592 | tf_op jit(solution)/shard_map/all_gather | solution.py:31
  13.4 56.9 %copy-start.5 = (bf16[512,256]{1,0:T(8,128)(2,1)S(1)}, bf16[512,256]{1,0:T(8,128)(2,1)}, u32[]{:S(2)}) copy-start(bf16[512,256]{1,0:T(8,128)(2,1)} %param.9) | copy-start | bytes 786436
  13.4 89.9 %reduce-scatter.2.cloned.1.call-start = ((), (), s32[]{:S(2)}) async-start(), calls=%async_computation.2 | async-start | bytes 1179648 | tf_op jit(solution)/shard_map/reduce_scatter | solution.py:34
  69.3 1.0 copy-start.2
  71.7 271.0 %all-reduce.3.cloned.1.call-start = ((), (), s32[]{:S(2)}) async-start(), calls=%async_computation.3 | async-start | bytes 9437184 | tf_op jit(solution)/shard_map/psum | solution.py:110
  105.3 57.9 %copy-start.6 = (s32[128]{0:T(128)S(1)}, s32[128]{0:T(128)}, u32[]{:S(2)}) copy-start(s32[128]{0:T(128)} %param.7) | copy-start | bytes 1540
  120.3 15.1 %collective-permute-start = (bf16[1024,256]{1,0:T(8,128)(2,1)S(1)}, bf16[1024,256]{1,0:T(8,128)(2,1)S(1)}, u32[]{:S(2)}, u32[]{:S(2)}) collective-permute-start(bf16[1024,256]{1,0:T(8,128)(2,1)S(1)} %all_gather.13), channel_id=1, source_target_pairs={{24,0},{0,8},{8,16},{16,24},{25,1},{1,9},{9,17},{17,25},{26,2},{2,... | collective-permute-start | bytes 1572872 | tf_op jit(solution)/shard_map/ppermute | solution.py:13
  135.4 14.3 %collective-permute-start.1 = (bf16[1024,256]{1,0:T(8,128)(2,1)S(1)}, bf16[1024,256]{1,0:T(8,128)(2,1)}, u32[]{:S(2)}, u32[]{:S(2)}) collective-permute-start(bf16[1024,256]{1,0:T(8,128)(2,1)S(1)} %collective-permute-done), channel_id=1, source_target_pairs={{24,0},{0,8},{8,16},{16,24},{25,1},{1,9},{9,17},{17,25},{26,2},{2,... | collective-permute-start | bytes 1572872 | tf_op jit(solution)/shard_map/ppermute | solution.py:13
  149.7 13.6 %collective-permute-start.2 = (bf16[1024,256]{1,0:T(8,128)(2,1)}, bf16[1024,256]{1,0:T(8,128)(2,1)S(1)}, u32[]{:S(2)}, u32[]{:S(2)}) collective-permute-start(bf16[1024,256]{1,0:T(8,128)(2,1)} %collective-permute-done.1), channel_id=1, source_target_pairs={{24,0},{0,8},{8,16},{16,24},{25,1},{1,9},{9,17},{17,25},{26,2},{2,... | collective-permute-start | bytes 1572872 | tf_op jit(solution)/shard_map/ppermute | solution.py:13
  204.0 2.1 copy-start.1
  205.7 15.8 %copy-start.3 = (bf16[1024,512]{1,0:T(8,128)(2,1)S(1)}, bf16[1024,512]{1,0:T(8,128)(2,1)}, u32[]{:S(2)}) copy-start(bf16[1024,512]{1,0:T(8,128)(2,1)} %copy-done.2) | copy-start | bytes 3145732
  342.7 4.7 %copy-start.4 = (f32[512,256]{1,0:T(8,128)S(1)}, f32[512,256]{1,0:T(8,128)}, u32[]{:S(2)}) copy-start(f32[512,256]{1,0:T(8,128)} %get-tuple-element.36) | copy-start | bytes 1572868
Sparse Core Ops, SparseCore 0:
  13.5 49.5 all-gather.2
  71.8 31.4 reduce-scatter.1
  231.5 111.1 all-reduce.2
where the time goes:
time: 356 us
  waiting for transfers between devices  193 us (54%)
  blocking collectives  105 us (29%)
  matrix products  28.4 us (8%)
  between operations  15.7 us (4%)
  local copies, waits for them, and re-layouts  6.53 us (2%)
  other arithmetic  5.44 us (2%)
    psum x1, waiting for transfers between devices, shards(): first_grad, second_grad = lax.psum((first_grad, second_grad), 'blk')  72.4 us
    all_gather x1, waiting for transfers between devices, shards(): pooled_all = lax.all_gather(pooled, 'grp', axis=0, tiled=True)  49.7 us
    ppermute x3, waiting for transfers between devices, shifted(): return lax.ppermute(block, axis, route)  39 us
    psum x1, blocking collectives, shards(): lax.psum(jnp.sum(log_norm - pos_score), ('blk', 'grp'))  38.3 us
    all_gather x1, blocking collectives, shards(): every_norm = lax.all_gather(log_norm, ('blk', 'grp'), axis=0, tiled=True)  36.9 us
    reduce_scatter x1, waiting for transfers between devices, shards(): lax.psum_scatter(jnp.dot(hidden, w_second, preferred_element_type=jnp.flo...  31.5 us
    all_gather x1, blocking collectives, shards(): key_block = lax.all_gather(lower_match_vectors, 'grp', axis=0, tiled=True)  14.9 us
    all_gather x1, blocking collectives, shards(): group_grad = lax.all_gather(raw_grad, 'grp', axis=0, tiled=True)  14.9 us
  transfers between devices with their start and end apart: 6, of which 6 were waited for; matrix products, arithmetic and copies ran while one was open for 1% of the time, Pallas kernels for 0%

commit v1 on v0

v1 whole, which is shorter than its diff:
```python
import functools

import jax
import jax.numpy as jnp
from jax import lax
from jax.experimental import pallas as pl
from jax.experimental.pallas import tpu as pltpu
from jax.sharding import PartitionSpec as P

sharpness = 20.0
score_top = 20.0
MESH = pl.DeviceIdType.MESH
F32 = jnp.float32
BF16 = jnp.bfloat16


def aligned(start, step):
    return pl.multiple_of(start, step)


def greet(partners):
    barrier = pltpu.get_barrier_semaphore()
    for device in partners:
        pl.semaphore_signal(barrier, inc=1, device_id=device, device_id_type=MESH)
    pl.semaphore_wait(barrier, len(partners))


def remote(src, dst, send_sem, recv_sem, device):
    return pltpu.make_async_remote_copy(
        src_ref=src,
        dst_ref=dst,
        send_sem=send_sem,
        recv_sem=recv_sem,
        device_id=device,
        device_id_type=MESH,
    )


def head_kernel(
    n, pooled_ref, first_ref, second_ref, all_ref, preact_ref, hidden_ref, partial_ref,
    ring_send, ring_recv, pair_send, pair_recv,
):
    rows = pooled_ref.shape[0]
    half = rows // 2
    steps = n // 2
    g = lax.axis_index("grp")
    z, c = g // 2, g % 2
    pair = {"grp": z * 2 + 1 - c}
    right = {"grp": ((z + 1) % n) * 2 + c}
    left = {"grp": ((z + n - 1) % n) * 2 + c}
    greet([pair, right, left])

    def block(chip, core, start=0, size=rows):
        return all_ref.at[pl.ds(aligned((chip * 2 + core) * rows + start, half), size)]

    def ring_copy(direction, s):
        chip = (z - s + n) % n if direction == 0 else (z + s) % n
        start, size = (0, rows) if s + 1 < steps else (direction * half, half)
        dst = block(chip, c, start, size)
        src = pooled_ref.at[pl.ds(start, size)] if s == 0 else dst
        return remote(
            src, dst, ring_send.at[direction, s], ring_recv.at[direction, s],
            right if direction == 0 else left,
        )

    def pair_copy(k, chip):
        dst = block(chip, c)
        src = pooled_ref if k == 0 else dst
        return remote(src, dst, pair_send.at[k], pair_recv.at[k], pair)

    def head(chip, core, own=False):
        span = pl.ds(aligned((chip * 2 + core) * rows, rows), rows)
        features = pooled_ref[...] if own else all_ref[span, :]
        if own:
            all_ref[span, :] = features
        preact = jnp.dot(features, first_ref[...], preferred_element_type=F32)
        preact_ref[span, :] = preact
        hidden = jax.nn.gelu(preact).astype(BF16)
        hidden_ref[span, :] = hidden
        partial_ref[span, :] = jnp.dot(hidden, second_ref[...], preferred_element_type=F32)

    started = []

    def start(copy):
        copy.start()
        started.append(copy)
        return copy

    rights = [start(ring_copy(0, 0))]
    lefts = [start(ring_copy(1, 0))]
    pairs = [(start(pair_copy(0, z)), z)]
    head(z, c, own=True)
    waited = 0
    for s in range(steps):
        rights[s].wait_recv()
        lefts[s].wait_recv()
        before = (z - 1 - s + 2 * n) % n
        after = (z + 1 + s) % n
        if s + 1 < steps:
            rights.append(start(ring_copy(0, s + 1)))
            lefts.append(start(ring_copy(1, s + 1)))
            fresh = [before, after]
        else:
            fresh = [after]
        arrived = pairs[waited:]
        waited = len(pairs)
        for chip in fresh:
            pairs.append((start(pair_copy(len(pairs), chip)), chip))
        for copy, chip in arrived:
            copy.wait_recv()
            head(chip, 1 - c)
        for chip in fresh:
            head(chip, c)
    for copy, chip in pairs[waited:]:
        copy.wait_recv()
        head(chip, 1 - c)
    for copy in started:
        copy.wait_send()


def middle_kernel(
    cycle, n, part_ref, pos_ref, grad_ref, loss_ref,
    pbuf, acc, zbuf, unit_ref, length_ref, keys, stats, escore,
    psend, precv, zsend, zrecv, ksend, krecv, ssend, srecv, gsend, grecv,
):
    group = 2 * n
    count = cycle * group
    rows, width = unit_ref.shape
    b = lax.axis_index("blk")
    g = lax.axis_index("grp")
    z, c = g // 2, g % 2
    me = b * group + g
    pair_g = z * 2 + 1 - c

    def other(k):
        device = (me + k) % count
        return {"blk": device // group, "grp": device % group}

    barrier = pltpu.get_barrier_semaphore()

    def hello(k, carry):
        pl.semaphore_signal(barrier, inc=1, device_id=other(k), device_id_type=MESH)
        return carry

    lax.fori_loop(1, count, hello, 0)
    pl.semaphore_wait(barrier, count - 1)

    started = []

    def start(copy):
        copy.start()
        started.append(copy)
        return copy

    def part(chip, core):
        return pl.ds(aligned((chip * 2 + core) * rows, rows), rows)

    order = list(range(1, n)) + [0]
    fromers = {}
    for d in order:
        fromers[d] = start(
            remote(
                part_ref.at[part((z + d) % n, 1 - c)], pbuf.at[d],
                psend.at[d], precv.at[d], {"grp": pair_g},
            )
        )
    sums = {}
    for d in order:
        fromers[d].wait_recv()
        total = part_ref[part((z + d) % n, c), :] + pbuf[d]
        acc[d] = total
        if d:
            sums[d] = start(
                remote(
                    acc.at[d], zbuf.at[d], zsend.at[d], zrecv.at[d],
                    {"grp": ((z + d) % n) * 2 + c},
                )
            )
    raw = acc[0]
    for d in range(1, n):
        sums[d].wait_recv()
        raw = raw + zbuf[d]
    length = jnp.sqrt(jnp.sum(raw * raw, axis=1, keepdims=True) + 1e-06)
    unit = raw / length
    unit_ref[...] = unit
    length_ref[...] = jnp.broadcast_to(length, length_ref.shape)
    keys[me] = unit.astype(BF16)

    def slot(e, d, core):
        return ((b - e + cycle) % cycle * n + (z - d + n) % n) * 2 + core

    sent = [0]

    def send(s, device):
        k = sent[0]
        sent[0] += 1
        return start(remote(keys.at[s], keys.at[s], ksend.at[k], krecv.at[s], device))

    def arrive(s):
        remote(keys.at[s], keys.at[s], ksend.at[0], krecv.at[s], {"grp": pair_g}).wait_recv()

    for d in range(1, n):
        send(me, {"grp": ((z + d) % n) * 2 + c})
    for e in range(1, cycle):
        send(me, {"blk": (b + e) % cycle})
    send(me, {"grp": pair_g})
    for d in range(1, n):
        s = slot(0, d, c)
        arrive(s)
        for e in range(1, cycle):
            send(s, {"blk": (b + e) % cycle})
        send(s, {"grp": pair_g})
    for d in range(n):
        for e in range(1, cycle):
            s = slot(e, d, c)
            arrive(s)
            send(s, {"grp": pair_g})
    for d in range(n):
        for e in range(cycle):
            arrive(slot(e, d, 1 - c))

    lane = 128
    per = 4
    chunk = per * rows
    row_ids = me * rows + lax.broadcasted_iota(jnp.int32, (rows, 1), 0)
    positive = pos_ref[...]
    mine = keys[me]

    def key_ids(j):
        return j * chunk + lax.broadcasted_iota(jnp.int32, (1, chunk), 1)

    def lanes(values):
        folded = values[:, :lane]
        for t in range(1, chunk // lane):
            folded = folded + values[:, t * lane : (t + 1) * lane]
        return folded

    def first_pass(j, carry):
        total, pos_score = carry
        block = keys[pl.ds(j * per, per)].reshape(chunk, width)
        scores = (
            lax.dot_general(mine, block, (((1,), (1,)), ((), ())), preferred_element_type=F32)
            * sharpness
        )
        ids = key_ids(j)
        terms = jnp.where(ids == row_ids, 0.0, jnp.exp(scores - score_top))
        escore[:, pl.ds(aligned(j * chunk, chunk), chunk)] = terms
        picked = jnp.where(ids == positive, scores, 0.0)
        return total + lanes(terms), pos_score + lanes(picked)

    zero = jnp.zeros((rows, lane), F32)
    total, pos_score = lax.fori_loop(0, count // per, first_pass, (zero, zero))
    total = jnp.sum(total, axis=1, keepdims=True)
    inverse = 1.0 / total
    term = jnp.log(total) + score_top - jnp.sum(pos_score, axis=1, keepdims=True)
    eye = lax.broadcasted_iota(jnp.int32, (rows, rows), 0) == lax.broadcasted_iota(
        jnp.int32, (rows, rows), 1
    )
    inverse_row = jnp.sum(jnp.where(eye, inverse, 0.0), axis=0, keepdims=True)
    term_row = jnp.sum(jnp.where(eye, term, 0.0), axis=0, keepdims=True)
    which = lax.broadcasted_iota(jnp.int32, (8, rows), 0)
    stats[me] = jnp.where(which == 0, inverse_row, term_row)

    def stat_copy(k, s):
        return remote(stats.at[s], stats.at[s], ssend.at[k], srecv.at[s], other(k))

    def tell(k, carry):
        stat_copy(k, me).start()
        return carry

    lax.fori_loop(1, count, tell, 0)

    def second_pass(j, gradient):
        span = pl.ds(aligned(j * chunk, chunk), chunk)
        block = keys[pl.ds(j * per, per)].reshape(chunk, width)
        paired = jnp.where(key_ids(j) == positive, 1.0, 0.0)
        weights = (escore[:, span] * inverse - paired).astype(BF16)
        return gradient + jnp.dot(weights, block, preferred_element_type=F32)

    gradient = lax.fori_loop(0, count // per, second_pass, jnp.zeros((rows, width), F32))

    def hear(k, carry):
        stat_copy(k, (me - k + count) % count).wait_recv()
        stat_copy(k, me).wait_send()
        return carry

    lax.fori_loop(1, count, hear, 0)
    loss = jnp.sum(jnp.sum(stats[:, 1, :], axis=0, keepdims=True), axis=1, keepdims=True)
    loss_ref[...] = jnp.broadcast_to(loss / (count * rows), loss_ref.shape)

    def mirror_pass(j, gradient):
        span = pl.ds(aligned(j * chunk, chunk), chunk)
        block = keys[pl.ds(j * per, per)].reshape(chunk, width)
        paired = jnp.where(key_ids(j) == positive, 1.0, 0.0)
        scale = jnp.concatenate([stats[j * per + t, 0:1, :] for t in range(per)], axis=1)
        weights = (escore[:, span] * scale - paired).astype(BF16)
        return gradient + jnp.dot(weights, block, preferred_element_type=F32)

    mirrored = lax.fori_loop(0, count // per, mirror_pass, jnp.zeros((rows, width), F32))
    sphere = (gradient + mirrored) * (sharpness / (count * rows))
    unit = unit_ref[...]
    raw_grad = (sphere - unit * jnp.sum(unit * sphere, axis=1, keepdims=True)) / length_ref[:, 0:1]
    grad_ref[part(z, c), :] = raw_grad.astype(BF16)

    def grad_copy(chip, k, q, device):
        span = part(chip, c)
        return start(remote(grad_ref.at[span], grad_ref.at[span], gsend.at[k], grecv.at[q], device))

    others = []
    for d in range(1, n):
        others.append(grad_copy(z, d, d, {"grp": ((z + d) % n) * 2 + c}))
    pairs = [grad_copy(z, n, n, {"grp": pair_g})]
    for d in range(1, n):
        others[d - 1].wait_recv()
        pairs.append(grad_copy((z - d + n) % n, n + d, n + d, {"grp": pair_g}))
    for copy in pairs:
        copy.wait_recv()
    for copy in started:
        copy.wait_send()


def reduce_kernel(
    cycle, lane_count, first_ref, second_ref, out_ref, acc, sendb, recvb,
    rs_send, rs_recv, ag_send, ag_recv,
):
    b = lax.axis_index("blk")
    stages = cycle.bit_length() - 1
    bits = [(b // (1 << t)) % 2 for t in range(stages)]
    peers = [{"blk": b + (1 - 2 * bits[t]) * (1 << t)} for t in range(stages)]
    greet(peers)
    top = first_ref.shape[0]
    total = out_ref.shape[0]
    acc[pl.ds(0, top), :] = first_ref[...]
    acc[pl.ds(top, total - top), :] = second_ref[...]
    size = total // lane_count
    orders = [
        list(range(stages)) if lane % 2 == 0 else list(range(stages))[::-1]
        for lane in range(lane_count)
    ]
    current = [lane * size for lane in range(lane_count)]
    kept = [[None] * stages for _ in range(lane_count)]
    copies = {}
    finals = {}
    started = []

    def span(start, length):
        return pl.ds(aligned(start, 16), length)

    def offset(lane, i):
        return lane * size + size - (size >> i)

    def start_reduce(lane, i):
        t = orders[lane][i]
        length = size >> (i + 1)
        away = current[lane] + (1 - bits[t]) * length
        current[lane] = current[lane] + bits[t] * length
        kept[lane][i] = current[lane]
        buffer = pl.ds(offset(lane, i), length)
        sendb[buffer, :] = acc[span(away, length), :].astype(BF16)
        copy = remote(
            sendb.at[buffer], recvb.at[buffer], rs_send.at[lane, i], rs_recv.at[lane, i], peers[t]
        )
        copy.start()
        started.append(copy)
        copies[lane, i] = copy

    def start_gather(lane, i):
        t = orders[lane][i]
        rows = out_ref.at[span(kept[lane][i], size >> (i + 1))]
        copy = remote(rows, rows, ag_send.at[lane, i], ag_recv.at[lane, i], peers[t])
        copy.start()
        started.append(copy)
        finals[lane, i] = copy

    for lane in range(lane_count):
        start_reduce(lane, 0)
    for i in range(stages):
        for lane in range(lane_count):
            copies[lane, i].wait_recv()
            length = size >> (i + 1)
            keep = span(kept[lane][i], length)
            summed = acc[keep, :] + recvb[pl.ds(offset(lane, i), length), :].astype(F32)
            if i + 1 < stages:
                acc[keep, :] = summed
                start_reduce(lane, i + 1)
            else:
                out_ref[keep, :] = summed.astype(BF16)
                start_gather(lane, i)
    for i in reversed(range(stages)):
        for lane in range(lane_count):
            finals[lane, i].wait_recv()
            if i:
                start_gather(lane, i - 1)
    for copy in started:
        copy.wait_send()


VMEM = pl.BlockSpec(memory_space=pltpu.VMEM)
DMA = pltpu.SemaphoreType.DMA


def params(number, mib=None):
    return pltpu.CompilerParams(
        collective_id=number,
        has_side_effects=True,
        vmem_limit_bytes=None if mib is None else mib << 20,
    )


def shards(frames, counts, positives, w_first, w_second):
    rows, slot_count, width = frames.shape
    cycle = lax.axis_size("blk")
    group = lax.axis_size("grp")
    n = group // 2
    count = cycle * group
    units, edge = w_second.shape
    frame_mask = (jnp.arange(slot_count, dtype=jnp.int32)[None, :] < counts[:, None]).astype(BF16)
    summed = jnp.einsum("rf,rfc->rc", frame_mask, frames, preferred_element_type=F32)
    pooled = (summed / counts[:, None].astype(F32)).astype(BF16)
    steps = n // 2
    pooled_all, preact, hidden, partial = pl.pallas_call(
        functools.partial(head_kernel, n),
        out_shape=(
            jax.ShapeDtypeStruct((group * rows, width), BF16),
            jax.ShapeDtypeStruct((group * rows, units), F32),
            jax.ShapeDtypeStruct((group * rows, units), BF16),
            jax.ShapeDtypeStruct((group * rows, edge), F32),
        ),
        in_specs=[VMEM] * 3,
        out_specs=(VMEM,) * 4,
        scratch_shapes=[DMA((2, steps)), DMA((2, steps)), DMA((n,)), DMA((n,))],
        compiler_params=params(0),
        name="head",
    )(pooled, w_first, w_second)
    group_grad, loss = pl.pallas_call(
        functools.partial(middle_kernel, cycle, n),
        out_shape=(
            jax.ShapeDtypeStruct((group * rows, edge), BF16),
            jax.ShapeDtypeStruct((8, 128), F32),
        ),
        in_specs=[VMEM] * 2,
        out_specs=(VMEM,) * 2,
        scratch_shapes=[
            pltpu.VMEM((n, rows, edge), F32),
            pltpu.VMEM((n, rows, edge), F32),
            pltpu.VMEM((n, rows, edge), F32),
            pltpu.VMEM((rows, edge), F32),
            pltpu.VMEM((rows, 128), F32),
            pltpu.VMEM((count, rows, edge), BF16),
            pltpu.VMEM((count, 8, rows), F32),
            pltpu.VMEM((rows, count * rows), F32),
            DMA((n,)), DMA((n,)), DMA((n,)), DMA((n,)),
            DMA((count,)), DMA((count,)), DMA((count,)), DMA((count,)),
            DMA((2 * n,)), DMA((2 * n,)),
        ],
        compiler_params=params(1),
        name="middle",
    )(partial, positives[:, None])
    second_grad = lax.dot_general(
        hidden, group_grad, (((0,), (0,)), ((), ())), preferred_element_type=F32
    )
    hidden_grad = lax.dot_general(
        group_grad, w_second, (((1,), (1,)), ((), ())), preferred_element_type=F32
    )
    unused, backward = jax.vjp(jax.nn.gelu, preact)
    preact_grad = backward(hidden_grad)[0].astype(BF16)
    first_grad = lax.dot_general(
        pooled_all, preact_grad, (((0,), (0,)), ((), ())), preferred_element_type=F32
    )
    fold = units // edge
    folded_rows = units // fold
    folded = jnp.concatenate(
        [second_grad[t * folded_rows : (t + 1) * folded_rows] for t in range(fold)], axis=1
    )
    total = width + folded_rows
    lane_count = 4 if total % (4 * cycle * 16) == 0 else 2
    stages = cycle.bit_length() - 1
    summed = pl.pallas_call(
        functools.partial(reduce_kernel, cycle, lane_count),
        out_shape=jax.ShapeDtypeStruct((total, units), BF16),
        in_specs=[VMEM] * 2,
        out_specs=VMEM,
        scratch_shapes=[
            pltpu.VMEM((total, units), F32),
            pltpu.VMEM((total, units), BF16),
            pltpu.VMEM((total, units), BF16),
            DMA((lane_count, stages)), DMA((lane_count, stages)),
            DMA((lane_count, stages)), DMA((lane_count, stages)),
        ],
        compiler_params=params(2),
        name="reduce",
    )(first_grad, folded)
    first_out = summed[:width].astype(F32)
    second_out = jnp.concatenate(
        [summed[width:, t * edge : (t + 1) * edge] for t in range(fold)], axis=0
    ).astype(F32)
    return (loss[0, 0], first_out, second_out)


def solution(mesh):
    return jax.shard_map(
        shards,
        mesh=mesh,
        in_specs=(
            P(("blk", "grp"), None, None),
            P(("blk", "grp")),
            P(("blk", "grp")),
            P(None, "grp"),
            P("grp", None),
        ),
        out_specs=(P(), P(None, "grp"), P("grp", None)),
        check_vma=False,
    )
```

time: 356 us -> 174 us (0.49)
  waiting for transfers between devices: 193 us -> 0 us
  Pallas kernels: 0 us -> 149 us
  blocking collectives: 105 us -> 0 us
  matrix products: 28.4 us -> 13.2 us
  between operations: 15.7 us -> 0.75 us
    pallas_call x0 -> x3, Pallas kernels: none -> 149 us  [the longest x1 55 us: shards(): pl.pallas_call(functools.partial(middle_kernel, cycle, n), out_shape=(jax...]
    psum x1 -> x0, waiting for transfers between devices: 72.4 us -> none  [shards(): first_grad, second_grad = lax.psum((first_grad, second_grad), 'blk')]
    all_gather x3 -> x0, blocking collectives: 66.7 us -> none  [the longest x1 36.9 us: shards(): every_norm = lax.all_gather(log_norm, ('blk', 'grp'), axis=0, tiled=True)]
    all_gather x1 -> x0, waiting for transfers between devices: 49.7 us -> none  [shards(): pooled_all = lax.all_gather(pooled, 'grp', axis=0, tiled=True)]
    ppermute x3 -> x0, waiting for transfers between devices: 39 us -> none  [shifted(): return lax.ppermute(block, axis, route)]
    psum x1 -> x0, blocking collectives: 38.3 us -> none  [shards(): lax.psum(jnp.sum(log_norm - pos_score), ('blk', 'grp'))]
    reduce_scatter x1 -> x0, waiting for transfers between devices: 31.5 us -> none  [shards(): lax.psum_scatter(jnp.dot(hidden, w_second, preferred_element_type=jnp.flo...]
    dot_general x15 -> x1, matrix products: 18.6 us -> 3.42 us  [shards(): jnp.einsum('rf,rfc->rc', frame_mask, frames, preferred_element_type=F32)]
  transfers between devices with their start and end apart: 6 -> 0, of which waited for: 6 -> 0; matrix products, arithmetic and copies ran while one was open for 1% -> 0% of each run, Pallas kernels for 0% -> 0%
where the time goes in v1:
time: 174 us; the launch traced here: 173 us
  Pallas kernels  149 us (86%)
  matrix products  13.2 us (8%)
  other arithmetic  7.77 us (4%)
  local copies, waits for them, and re-layouts  2.99 us (2%)
    pallas_call x1, Pallas kernels, shards(): pl.pallas_call(functools.partial(middle_kernel, cycle, n), out_shape=(jax...  55 us
    pallas_call x1, Pallas kernels, shards(): pl.pallas_call(functools.partial(head_kernel, n), out_shape=(jax.ShapeDty...  48.3 us
    pallas_call x1, Pallas kernels, shards(): pl.pallas_call(functools.partial(reduce_kernel, cycle, lane_count), out_s...  45.3 us
    dot_general x1, matrix products, shards(): lax.dot_general(pooled_all, preact_grad, (((0,), (0,)), ((), ())), prefer...  7.81 us
    convert_element_type x1, other arithmetic, shards(): first_out = summed[:width].astype(F32)  4.2 us

profile of v1, /device:TPU:0, one launch (start us, length us, event | category | flops | bytes accessed | tf_op | source)
XLA Modules:
  0.0 173.3 jit_solution(14349815866812365202)
XLA Ops:
  0.6 0.7 fusion.13
  1.4 0.0 copy-start.2
  1.4 3.4 %fusion.11 = f32[128,1,2048]{2,1,0:T(1,128)S(1)} fusion(bf16[128,8,2048]{2,1,0:T(8,128)(2,1)} %param.5, pred[128,8,1]{1,0,2:T(32,128)(4,1)S(1)} %fusion.13), kind=kOutput, calls=%fused_computation.17 | convolution fusion | flops 4194304 | bytes 5243904 | tf_op jit(solution)/shard_map/rf,rfc->rc/dot_general | solution.py:418
  4.8 0.0 copy-done.2
  4.8 0.0 copy-start.1
  4.8 1.1 fusion.7.pooled_ref
  6.0 48.3 %head.1 = (bf16[1024,2048]{1,0:T(8,128)(2,1)}, f32[1024,512]{1,0:T(8,128)}, bf16[1024,512]{1,0:T(8,128)(2,1)}, f32[1024,256]{1,0:T(8,128)}) custom-call(bf16[128,2048]{1,0:T(8,128)(2,1)} %fusion.7.pooled_ref, bf16[2048,512]{1,0:T(8,128)(2,1)} %first_ref.1, bf16[512,256]{1,0:T(8,128)(2,1)} %second_ref.1), custom_call_target="tpu_custom_call" | custom-call | tf_op jit(solution)/shard_map/head/pallas_call | solution.py:421
  54.3 0.0 copy-done.1
  54.3 0.7 copy.8.pos_ref
  55.0 55.0 %middle.1 = (bf16[1024,256]{1,0:T(8,128)(2,1)}, f32[8,128]{1,0:T(8,128)}) custom-call(f32[1024,256]{1,0:T(8,128)} %get-tuple-element.9.part_ref, s32[128,1]{1,0:T(8,128)} %copy.8.pos_ref), custom_call_target="tpu_custom_call" | custom-call | tf_op jit(solution)/shard_map/middle/pallas_call | solution.py:435
  110.0 0.0 copy-start
  110.0 0.0 copy-start.3
  110.0 0.0 copy-start.4
  110.0 2.0 %fusion.22 = f32[512,256]{1,0:T(8,128)S(1)} fusion(bf16[1024,512]{1,0:T(8,128)(2,1)} %get-tuple-element.14, bf16[1024,256]{1,0:T(8,128)(2,1)} %get-tuple-element.12), kind=kOutput, calls=%fused_computation.29 | convolution fusion | flops 268435456 | bytes 2097152 | tf_op jit(solution)/shard_map/dot_general | solution.py:459
  112.1 0.9 pad_maximum_fusion.second_ref
  112.9 0.0 copy-done
  112.9 0.0 copy-done.3
  112.9 0.0 copy-done.4
  112.9 7.8 %fusion.8.first_ref = f32[2048,512]{1,0:T(8,128)} fusion(bf16[1024,2048]{1,0:T(8,128)(2,1)} %get-tuple-element.11, f32[1024,512]{1,0:T(8,128)S(1)} %copy-done.3, bf16[1024,256]{1,0:T(8,128)(2,1)S(1)} %copy-done.4, bf16[512,256]{1,0:T(8,128)(2,1)S(1)} %copy-done), kind=kOutput, calls=%fused_computation.12 | convolution fusion | flops 2426404864 | bytes 11272192 | tf_op jit(solution)/shard_map/dot_general | solution.py:467
  120.7 45.3 %reduce.1 = bf16[2304,512]{1,0:T(8,128)(2,1)} custom-call(f32[2048,512]{1,0:T(8,128)} %fusion.8.first_ref, f32[256,512]{1,0:T(8,128)} %pad_maximum_fusion.second_ref), custom_call_target="tpu_custom_call" | custom-call | tf_op jit(solution)/shard_map/reduce/pallas_call | solution.py:478
  166.1 1.0 fusion.20
  167.1 0.8 maximum_convert_fusion
  167.9 4.2 %slice_convert_fusion = f32[2048,512]{1,0:T(8,128)} fusion(bf16[2304,512]{1,0:T(8,128)(2,1)} %reduce.1), kind=kLoop, calls=%fused_computation.9 | loop fusion | flops 1048576 | bytes 6291456 | tf_op jit(solution)/shard_map/convert_element_type | solution.py:493
  172.1 1.2 slice.18
  (2 shorter events, 0.0 us)
Async XLA Ops:
  1.4 3.4 %copy-start.2 = (s32[128]{0:T(128)S(1)}, s32[128]{0:T(128)}, u32[]{:S(2)}) copy-start(s32[128]{0:T(128)} %param.6) | copy-start | bytes 1540
  4.8 49.5 %copy-start.1 = (s32[128]{0:T(128)S(1)}, s32[128]{0:T(128)}, u32[]{:S(2)}) copy-start(s32[128]{0:T(128)} %param.7) | copy-start | bytes 1540
  110.0 2.9 %copy-start = (bf16[512,256]{1,0:T(8,128)(2,1)S(1)}, bf16[512,256]{1,0:T(8,128)(2,1)}, u32[]{:S(2)}) copy-start(bf16[512,256]{1,0:T(8,128)(2,1)} %second_ref.1) | copy-start | bytes 786436
  110.0 2.9 %copy-start.3 = (f32[1024,512]{1,0:T(8,128)S(1)}, f32[1024,512]{1,0:T(8,128)}, u32[]{:S(2)}) copy-start(f32[1024,512]{1,0:T(8,128)} %get-tuple-element.13) | copy-start | bytes 6291460
  110.0 2.9 %copy-start.4 = (bf16[1024,256]{1,0:T(8,128)(2,1)S(1)}, bf16[1024,256]{1,0:T(8,128)(2,1)}, u32[]{:S(2)}) copy-start(bf16[1024,256]{1,0:T(8,128)(2,1)} %get-tuple-element.12) | copy-start | bytes 1572868

commit v2 on v1

--- a/solution.py
+++ b/solution.py
@@ -37,39 +37,63 @@
 
 
 def head_kernel(
-    n, pooled_ref, first_ref, second_ref, all_ref, preact_ref, hidden_ref, partial_ref,
-    ring_send, ring_recv, pair_send, pair_recv,
+    n, pooled_ref, first_hbm, second_ref, all_out, preact_out, hidden_out, partial_ref,
+    first_ref, all_ref, preact_ref, hidden_ref,
+    line_send, line_recv, pair_send, pair_recv, load_sem, store_sem,
 ):
     rows = pooled_ref.shape[0]
-    half = rows // 2
-    steps = n // 2
+    parts = line_send.shape[2]
+    piece = rows // parts
     g = lax.axis_index("grp")
     z, c = g // 2, g % 2
     pair = {"grp": z * 2 + 1 - c}
-    right = {"grp": ((z + 1) % n) * 2 + c}
-    left = {"grp": ((z + n - 1) % n) * 2 + c}
-    greet([pair, right, left])
-
-    def block(chip, core, start=0, size=rows):
-        return all_ref.at[pl.ds(aligned((chip * 2 + core) * rows + start, half), size)]
-
-    def ring_copy(direction, s):
-        chip = (z - s + n) % n if direction == 0 else (z + s) % n
-        start, size = (0, rows) if s + 1 < steps else (direction * half, half)
-        dst = block(chip, c, start, size)
-        src = pooled_ref.at[pl.ds(start, size)] if s == 0 else dst
-        return remote(
-            src, dst, ring_send.at[direction, s], ring_recv.at[direction, s],
-            right if direction == 0 else left,
-        )
-
-    def pair_copy(k, chip):
-        dst = block(chip, c)
-        src = pooled_ref if k == 0 else dst
-        return remote(src, dst, pair_send.at[k], pair_recv.at[k], pair)
+    has_right, has_left = z < n - 1, z > 0
+    ways = (
+        ({"grp": g + 2}, has_right, lambda s: z - s, lambda s: z - 1 - s >= 0),
+        ({"grp": g - 2}, has_left, lambda s: z + s, lambda s: z + 1 + s < n),
+    )
+    load = pltpu.make_async_copy(first_hbm, first_ref, load_sem)
+    load.start()
+
+    barrier = pltpu.get_barrier_semaphore()
+    pl.semaphore_signal(barrier, inc=1, device_id=pair, device_id_type=MESH)
+    for device, exists, _, _ in ways:
+
+        @pl.when(exists)
+        def _():
+            pl.semaphore_signal(barrier, inc=1, device_id=device, device_id_type=MESH)
+
+    pl.semaphore_wait(barrier, 1 + has_right.astype(jnp.int32) + has_left.astype(jnp.int32))
+
+    def rows_of(chip, core):
+        return pl.ds(aligned((chip * 2 + core) * rows, rows), rows)
+
+    def spot(chip, q):
+        return all_ref.at[pl.ds(aligned((chip * 2 + c) * rows + q * piece, piece), piece)]
+
+    def line_copy(way, s, q, incoming=False):
+        device, _, chip, _ = ways[way]
+        dst = spot(chip(s + 1) if incoming else chip(s), q)
+        src = pooled_ref.at[pl.ds(q * piece, piece)] if s == 0 and not incoming else dst
+        return remote(src, dst, line_send.at[way, s, q], line_recv.at[way, s, q], device)
+
+    def pair_copy(k, chip, q):
+        dst = spot(chip, q)
+        src = pooled_ref.at[pl.ds(q * piece, piece)] if k == 0 else dst
+        return remote(src, dst, pair_send.at[k, q], pair_recv.at[k, q], pair)
+
+    def stores(chip, core):
+        span = rows_of(chip, core)
+        which = chip * 2 + core
+        return [
+            pltpu.make_async_copy(source.at[span], target.at[span], store_sem.at[i, which])
+            for i, (source, target) in enumerate(
+                ((all_ref, all_out), (preact_ref, preact_out), (hidden_ref, hidden_out))
+            )
+        ]
 
     def head(chip, core, own=False):
-        span = pl.ds(aligned((chip * 2 + core) * rows, rows), rows)
+        span = rows_of(chip, core)
         features = pooled_ref[...] if own else all_ref[span, :]
         if own:
             all_ref[span, :] = features
@@ -78,44 +102,89 @@
         hidden = jax.nn.gelu(preact).astype(BF16)
         hidden_ref[span, :] = hidden
         partial_ref[span, :] = jnp.dot(hidden, second_ref[...], preferred_element_type=F32)
-
-    started = []
-
-    def start(copy):
-        copy.start()
-        started.append(copy)
-        return copy
-
-    rights = [start(ring_copy(0, 0))]
-    lefts = [start(ring_copy(1, 0))]
-    pairs = [(start(pair_copy(0, z)), z)]
+        for copy in stores(chip, core):
+            copy.start()
+
+    def pair_head(k, chip):
+        for q in range(parts):
+            pair_copy(k, chip, q).wait_recv()
+        head(chip, 1 - c)
+
+    for q in range(parts):
+        for way in range(2):
+
+            @pl.when(ways[way][1])
+            def _():
+                line_copy(way, 0, q).start()
+
+        pair_copy(0, z, q).start()
+    load.wait()
     head(z, c, own=True)
-    waited = 0
-    for s in range(steps):
-        rights[s].wait_recv()
-        lefts[s].wait_recv()
-        before = (z - 1 - s + 2 * n) % n
-        after = (z + 1 + s) % n
-        if s + 1 < steps:
-            rights.append(start(ring_copy(0, s + 1)))
-            lefts.append(start(ring_copy(1, s + 1)))
-            fresh = [before, after]
-        else:
-            fresh = [after]
-        arrived = pairs[waited:]
-        waited = len(pairs)
-        for chip in fresh:
-            pairs.append((start(pair_copy(len(pairs), chip)), chip))
-        for copy, chip in arrived:
-            copy.wait_recv()
-            head(chip, 1 - c)
-        for chip in fresh:
-            head(chip, c)
-    for copy, chip in pairs[waited:]:
-        copy.wait_recv()
-        head(chip, 1 - c)
-    for copy in started:
-        copy.wait_send()
+
+    def key_of(way, s):
+        return 1 + s if way == 0 else n + s
+
+    for s in range(n - 1):
+        for q in range(parts):
+            for way in range(2):
+                _, exists, chip, arrives = ways[way]
+
+                @pl.when(arrives(s))
+                def _():
+                    line_copy(way, s, q, incoming=True).wait_recv()
+                    if s + 1 < n - 1:
+
+                        @pl.when(exists)
+                        def _():
+                            line_copy(way, s + 1, q).start()
+
+                    pair_copy(key_of(way, s), chip(s + 1), q).start()
+
+        if s == 0:
+            pair_head(0, z)
+        for way in range(2):
+            _, _, chip, arrives = ways[way]
+            if s:
+
+                @pl.when(arrives(s - 1))
+                def _():
+                    pair_head(key_of(way, s - 1), chip(s))
+
+            @pl.when(arrives(s))
+            def _():
+                head(chip(s + 1), c)
+
+    for way in range(2):
+        _, exists, chip, arrives = ways[way]
+
+        @pl.when(arrives(n - 2))
+        def _():
+            pair_head(key_of(way, n - 2), chip(n - 1))
+
+    for q in range(parts):
+        pair_copy(0, z, q).wait_send()
+        for way in range(2):
+            _, exists, chip, arrives = ways[way]
+
+            @pl.when(exists)
+            def _():
+                line_copy(way, 0, q).wait_send()
+
+            for s in range(n - 1):
+
+                @pl.when(arrives(s))
+                def _():
+                    pair_copy(key_of(way, s), chip(s + 1), q).wait_send()
+                    if s + 1 < n - 1:
+
+                        @pl.when(exists)
+                        def _():
+                            line_copy(way, s + 1, q).wait_send()
+
+    for chip in range(n):
+        for core in range(2):
+            for copy in stores(chip, core):
+                copy.wait()
 
 
 def middle_kernel(
@@ -210,20 +279,15 @@
         for e in range(1, cycle):
             send(s, {"blk": (b + e) % cycle})
         send(s, {"grp": pair_g})
-    for d in range(n):
-        for e in range(1, cycle):
-            s = slot(e, d, c)
-            arrive(s)
-            send(s, {"grp": pair_g})
-    for d in range(n):
-        for e in range(cycle):
-            arrive(slot(e, d, 1 - c))
-
     lane = 128
     per = 4
     chunk = per * rows
     row_ids = me * rows + lax.broadcasted_iota(jnp.int32, (rows, 1), 0)
-    positive = pos_ref[...]
+    eye = lax.broadcasted_iota(jnp.int32, (rows, rows), 0) == lax.broadcasted_iota(
+        jnp.int32, (rows, rows), 1
+    )
+    positive = jnp.sum(jnp.where(eye, pos_ref[...].astype(F32), 0.0), axis=1, keepdims=True)
+    positive = positive.astype(jnp.int32)
     mine = keys[me]
 
     def key_ids(j):
@@ -249,13 +313,23 @@
         return total + lanes(terms), pos_score + lanes(picked)
 
     zero = jnp.zeros((rows, lane), F32)
-    total, pos_score = lax.fori_loop(0, count // per, first_pass, (zero, zero))
+    carry = (zero, zero)
+    chunks = group // per
+    for e in range(cycle):
+        if e == 1:
+            for other_e in range(1, cycle):
+                for d in range(n):
+                    s = slot(other_e, d, c)
+                    arrive(s)
+                    send(s, {"grp": pair_g})
+        for d in range(n):
+            arrive(slot(e, d, 1 - c))
+        base = (b - e + cycle) % cycle * chunks
+        carry = lax.fori_loop(base, base + chunks, first_pass, carry)
+    total, pos_score = carry
     total = jnp.sum(total, axis=1, keepdims=True)
     inverse = 1.0 / total
     term = jnp.log(total) + score_top - jnp.sum(pos_score, axis=1, keepdims=True)
-    eye = lax.broadcasted_iota(jnp.int32, (rows, rows), 0) == lax.broadcasted_iota(
-        jnp.int32, (rows, rows), 1
-    )
     inverse_row = jnp.sum(jnp.where(eye, inverse, 0.0), axis=0, keepdims=True)
     term_row = jnp.sum(jnp.where(eye, term, 0.0), axis=0, keepdims=True)
     which = lax.broadcasted_iota(jnp.int32, (8, rows), 0)
@@ -285,8 +359,7 @@
         return carry
 
     lax.fori_loop(1, count, hear, 0)
-    loss = jnp.sum(jnp.sum(stats[:, 1, :], axis=0, keepdims=True), axis=1, keepdims=True)
-    loss_ref[...] = jnp.broadcast_to(loss / (count * rows), loss_ref.shape)
+    loss_ref[0, 0] = jnp.sum(stats[:, 1, :]) / (count * rows)
 
     def mirror_pass(j, gradient):
         span = pl.ds(aligned(j * chunk, chunk), chunk)
@@ -320,19 +393,67 @@
 
 
 def reduce_kernel(
-    cycle, lane_count, first_ref, second_ref, out_ref, acc, sendb, recvb,
-    rs_send, rs_recv, ag_send, ag_recv,
+    cycle, lane_count, grad_ref, second_ref, pooled_hbm, preact_hbm, hidden_hbm, out_ref,
+    pooled_ref, preact_ref, hidden_ref, back_ref, second_grad, acc, sendb, recvb,
+    load_sem, rs_send, rs_recv, ag_send, ag_recv,
 ):
+    loads = [
+        pltpu.make_async_copy(source, target, load_sem.at[i])
+        for i, (source, target) in enumerate(
+            ((preact_hbm, preact_ref), (hidden_hbm, hidden_ref), (pooled_hbm, pooled_ref))
+        )
+    ]
+    for load in loads:
+        load.start()
     b = lax.axis_index("blk")
     stages = cycle.bit_length() - 1
     bits = [(b // (1 << t)) % 2 for t in range(stages)]
     peers = [{"blk": b + (1 - 2 * bits[t]) * (1 << t)} for t in range(stages)]
     greet(peers)
-    top = first_ref.shape[0]
+    clips = preact_ref.shape[0]
+    edge = second_ref.shape[1]
+    fold = second_ref.shape[0] // edge
     total = out_ref.shape[0]
-    acc[pl.ds(0, top), :] = first_ref[...]
-    acc[pl.ds(top, total - top), :] = second_ref[...]
     size = total // lane_count
+    unit = size // cycle
+    top = pooled_ref.shape[1] // (lane_count * cycle)
+    low = unit - top
+    loads[0].wait()
+    step = 128
+
+    def back(i, carry):
+        span = pl.ds(aligned(i * step, step), step)
+        hidden_grad = lax.dot_general(
+            grad_ref[span, :], second_ref[...], (((1,), (1,)), ((), ())),
+            preferred_element_type=F32,
+        )
+        unused, backward = jax.vjp(jax.nn.gelu, preact_ref[span, :])
+        back_ref[span, :] = backward(hidden_grad)[0].astype(BF16)
+        return carry
+
+    lax.fori_loop(0, clips // step, back, 0)
+    loads[1].wait()
+    across = (((0,), (0,)), ((), ()))
+    second_grad[...] = lax.dot_general(
+        hidden_ref[...], grad_ref[...], across, preferred_element_type=F32
+    )
+    loads[2].wait()
+
+    def produce(lane):
+        wide = top * cycle
+        first = lax.dot_general(
+            pooled_ref[:, lane * wide : (lane + 1) * wide], back_ref[...], across,
+            preferred_element_type=F32,
+        )
+        for j in range(cycle):
+            at = lane * size + j * unit
+            acc[pl.ds(at, top), :] = first[j * top : (j + 1) * top]
+            for t in range(fold):
+                row = t * edge + (lane * cycle + j) * low
+                acc[pl.ds(at + top, low), t * edge : (t + 1) * edge] = second_grad[
+                    pl.ds(row, low), :
+                ]
+
     orders = [
         list(range(stages)) if lane % 2 == 0 else list(range(stages))[::-1]
         for lane in range(lane_count)
@@ -373,6 +494,7 @@
         finals[lane, i] = copy
 
     for lane in range(lane_count):
+        produce(lane)
         start_reduce(lane, 0)
     for i in range(stages):
         for lane in range(lane_count):
@@ -395,7 +517,23 @@
         copy.wait_send()
 
 
+def tail_kernel(unit, fold, sum_ref, loss_ref, first_ref, second_ref, out_ref):
+    block = sum_ref[...].astype(F32)
+    low = second_ref.shape[1] // (block.shape[0] // unit)
+    edge = second_ref.shape[2]
+    top = unit - low
+    for j in range(block.shape[0] // unit):
+        first_ref[j * top : (j + 1) * top, :] = block[j * unit : j * unit + top]
+        for t in range(fold):
+            second_ref[t, j * low : (j + 1) * low, :] = block[
+                j * unit + top : (j + 1) * unit, t * edge : (t + 1) * edge
+            ]
+    out_ref[0, 0] = loss_ref[0, 0]
+
+
 VMEM = pl.BlockSpec(memory_space=pltpu.VMEM)
+SMEM = pl.BlockSpec(memory_space=pltpu.SMEM)
+ANY = pl.BlockSpec(memory_space=pl.ANY)
 DMA = pltpu.SemaphoreType.DMA
 
 
@@ -417,7 +555,6 @@
     frame_mask = (jnp.arange(slot_count, dtype=jnp.int32)[None, :] < counts[:, None]).astype(BF16)
     summed = jnp.einsum("rf,rfc->rc", frame_mask, frames, preferred_element_type=F32)
     pooled = (summed / counts[:, None].astype(F32)).astype(BF16)
-    steps = n // 2
     pooled_all, preact, hidden, partial = pl.pallas_call(
         functools.partial(head_kernel, n),
         out_shape=(
@@ -426,9 +563,16 @@
             jax.ShapeDtypeStruct((group * rows, units), BF16),
             jax.ShapeDtypeStruct((group * rows, edge), F32),
         ),
-        in_specs=[VMEM] * 3,
-        out_specs=(VMEM,) * 4,
-        scratch_shapes=[DMA((2, steps)), DMA((2, steps)), DMA((n,)), DMA((n,))],
+        in_specs=[VMEM, ANY, VMEM],
+        out_specs=(ANY, ANY, ANY, VMEM),
+        scratch_shapes=[
+            pltpu.VMEM((width, units), BF16),
+            pltpu.VMEM((group * rows, width), BF16),
+            pltpu.VMEM((group * rows, units), F32),
+            pltpu.VMEM((group * rows, units), BF16),
+            DMA((2, n, 2)), DMA((2, n, 2)), DMA((2 * n, 2)), DMA((2 * n, 2)),
+            DMA, DMA((3, group)),
+        ],
         compiler_params=params(0),
         name="head",
     )(pooled, w_first, w_second)
@@ -436,10 +580,10 @@
         functools.partial(middle_kernel, cycle, n),
         out_shape=(
             jax.ShapeDtypeStruct((group * rows, edge), BF16),
-            jax.ShapeDtypeStruct((8, 128), F32),
+            jax.ShapeDtypeStruct((1, 1), F32),
         ),
         in_specs=[VMEM] * 2,
-        out_specs=(VMEM,) * 2,
+        out_specs=(VMEM, SMEM),
         scratch_shapes=[
             pltpu.VMEM((n, rows, edge), F32),
             pltpu.VMEM((n, rows, edge), F32),
@@ -455,46 +599,50 @@
         ],
         compiler_params=params(1),
         name="middle",
-    )(partial, positives[:, None])
-    second_grad = lax.dot_general(
-        hidden, group_grad, (((0,), (0,)), ((), ())), preferred_element_type=F32
-    )
-    hidden_grad = lax.dot_general(
-        group_grad, w_second, (((1,), (1,)), ((), ())), preferred_element_type=F32
-    )
-    unused, backward = jax.vjp(jax.nn.gelu, preact)
-    preact_grad = backward(hidden_grad)[0].astype(BF16)
-    first_grad = lax.dot_general(
-        pooled_all, preact_grad, (((0,), (0,)), ((), ())), preferred_element_type=F32
-    )
+    )(partial, positives[None, :])
     fold = units // edge
-    folded_rows = units // fold
-    folded = jnp.concatenate(
-        [second_grad[t * folded_rows : (t + 1) * folded_rows] for t in range(fold)], axis=1
-    )
-    total = width + folded_rows
-    lane_count = 4 if total % (4 * cycle * 16) == 0 else 2
+    total = width + units // fold
+    lane_count = 4 if units // fold % (4 * cycle * 16) == 0 else 2
     stages = cycle.bit_length() - 1
+    links = (lane_count, stages)
     summed = pl.pallas_call(
         functools.partial(reduce_kernel, cycle, lane_count),
         out_shape=jax.ShapeDtypeStruct((total, units), BF16),
-        in_specs=[VMEM] * 2,
+        in_specs=[VMEM, VMEM, ANY, ANY, ANY],
         out_specs=VMEM,
         scratch_shapes=[
+            pltpu.VMEM((group * rows, width), BF16),
+            pltpu.VMEM((group * rows, units), F32),
+            pltpu.VMEM((group * rows, units), BF16),
+            pltpu.VMEM((group * rows, units), BF16),
+            pltpu.VMEM((units, edge), F32),
             pltpu.VMEM((total, units), F32),
             pltpu.VMEM((total, units), BF16),
             pltpu.VMEM((total, units), BF16),
-            DMA((lane_count, stages)), DMA((lane_count, stages)),
-            DMA((lane_count, stages)), DMA((lane_count, stages)),
+            DMA((3,)), DMA(links), DMA(links), DMA(links), DMA(links),
         ],
         compiler_params=params(2),
         name="reduce",
-    )(first_grad, folded)
-    first_out = summed[:width].astype(F32)
-    second_out = jnp.concatenate(
-        [summed[width:, t * edge : (t + 1) * edge] for t in range(fold)], axis=0
-    ).astype(F32)
-    return (loss[0, 0], first_out, second_out)
+    )(group_grad, w_second, pooled_all, preact, hidden)
+    unit = total // (lane_count * cycle)
+    tiles = lane_count * cycle // 2
+    first_out, second_out, loss = pl.pallas_call(
+        functools.partial(tail_kernel, unit, fold),
+        grid=(tiles,),
+        out_shape=(
+            jax.ShapeDtypeStruct((width, units), F32),
+            jax.ShapeDtypeStruct((fold, units // fold, edge), F32),
+            jax.ShapeDtypeStruct((1, 1), F32),
+        ),
+        in_specs=[pl.BlockSpec((2 * unit, units), lambda i: (i, 0)), SMEM],
+        out_specs=(
+            pl.BlockSpec((width // tiles, units), lambda i: (i, 0)),
+            pl.BlockSpec((fold, units // fold // tiles, edge), lambda i: (0, i, 0)),
+            SMEM,
+        ),
+        name="tail",
+    )(summed, loss)
+    return (loss.reshape(()), first_out, second_out.reshape(units, edge))
 
 
 def solution(mesh):

time: 174 us -> 161 us (0.925)
  matrix products: 13.2 us -> 3.42 us
  other arithmetic: 7.77 us -> 2.54 us
  Pallas kernels: 149 us -> 154 us
  local copies, waits for them, and re-layouts: 2.99 us -> 0 us
    dot_general x2 -> x0, matrix products: 9.79 us -> none  [the longest x1 7.81 us: shards(): lax.dot_general(pooled_all, preact_grad, (((0,), (0,)), ((), ())), prefer...]
    pallas_call x0 -> x1, Pallas kernels: none -> 6.83 us  [shards(): pl.pallas_call(functools.partial(tail_kernel, unit, fold), grid=(tiles,),...]
    convert_element_type x2 -> x0, other arithmetic: 5.03 us -> none  [the longest x1 4.2 us: shards(): first_out = summed[:width].astype(F32)]
    pallas_call x1, Pallas kernels: 48.3 us -> 44.1 us  [shards(): pl.pallas_call(functools.partial(head_kernel, n), out_shape=(jax.ShapeDty...]
    pallas_call x1, Pallas kernels: 45.3 us -> 49.1 us  [shards(): pl.pallas_call(functools.partial(reduce_kernel, cycle, lane_count), out_s...]
    slice x3 -> x0, local copies, waits for them, and re-layouts: 2.22 us -> none  [the longest x1 1.19 us: shards(): return (loss[0, 0], first_out, second_out)]
where the time goes in v2:
time: 161 us; the launch traced here: 160 us
  Pallas kernels  154 us (96%)
  matrix products  3.42 us (2%)
  other arithmetic  2.54 us (2%)
    pallas_call x1, Pallas kernels, shards(): pl.pallas_call(functools.partial(middle_kernel, cycle, n), out_shape=(jax...  53.5 us
    pallas_call x1, Pallas kernels, shards(): pl.pallas_call(functools.partial(reduce_kernel, cycle, lane_count), out_s...  49.1 us
    pallas_call x1, Pallas kernels, shards(): pl.pallas_call(functools.partial(head_kernel, n), out_shape=(jax.ShapeDty...  44.1 us
    pallas_call x1, Pallas kernels, shards(): pl.pallas_call(functools.partial(tail_kernel, unit, fold), grid=(tiles,),...  6.83 us
    dot_general x1, matrix products, shards(): jnp.einsum('rf,rfc->rc', frame_mask, frames, preferred_element_type=F32)  3.42 us

profile of v2, /device:TPU:0, one launch (start us, length us, event | category | flops | bytes accessed | tf_op | source)
XLA Modules:
  0.0 160.1 jit_solution(17581252921552209920)
XLA Ops:
  0.6 0.7 convert_element_type.8
  1.3 0.7 fusion.3
  2.0 3.4 %fusion.1 = f32[128,1,2048]{2,1,0:T(1,128)S(1)} fusion(bf16[128,8,2048]{2,1,0:T(8,128)(2,1)} %param.5, pred[128,8,1]{1,0,2:T(32,128)(4,1)S(1)} %fusion.3), kind=kOutput, calls=%fused_computation.2 | convolution fusion | flops 4194304 | bytes 5243904 | tf_op jit(solution)/shard_map/rf,rfc->rc/dot_general | solution.py:556
  5.5 1.1 fusion.pooled_ref
  6.6 44.1 %head.1 = (bf16[1024,2048]{1,0:T(8,128)(2,1)}, f32[1024,512]{1,0:T(8,128)}, bf16[1024,512]{1,0:T(8,128)(2,1)}, f32[1024,256]{1,0:T(8,128)}) custom-call(bf16[128,2048]{1,0:T(8,128)(2,1)} %fusion.pooled_ref, bf16[2048,512]{1,0:T(8,128)(2,1)} %first_hbm.1, bf16[512,256]{1,0:T(8,128)(2,1)} %second_ref.3), custom_call_target="tpu_custom_call" | custom-call | tf_op jit(solution)/shard_map/head/pallas_call | solution.py:558
  50.7 53.5 %middle.1 = (bf16[1024,256]{1,0:T(8,128)(2,1)}, f32[1,1]{1,0:T(1,128)}) custom-call(f32[1024,256]{1,0:T(8,128)} %get-tuple-element.12.part_ref, s32[1,128]{1,0:T(1,128)} %bitcast.10), custom_call_target="tpu_custom_call" | custom-call | tf_op jit(solution)/shard_map/middle/pallas_call | solution.py:579
  104.2 49.1 %reduce.1.sum_ref = bf16[2304,512]{1,0:T(8,128)(2,1)} custom-call(bf16[1024,256]{1,0:T(8,128)(2,1)} %get-tuple-element.13.grad_ref, bf16[512,256]{1,0:T(8,128)(2,1)} %second_ref.3, bf16[1024,2048]{1,0:T(8,128)(2,1)} %get-tuple-element.14.pooled_hbm, f32[1024,512]{1,0:T(8,128)} %get-tuple-element.15.preact_hbm, bf16[1024,512]{1,0:T(8,128)(2,1)} %get-tuple-element.16.hidden_hbm), custom_call_target="tpu_custom_call" | custom-call | tf_op jit(solution)/shard_map/reduce/pallas_call | solution.py:608
  153.3 6.8 %tail.1 = (f32[2048,512]{1,0:T(8,128)}, f32[2,256,256]{2,1,0:T(8,128)}, f32[1,1]{1,0:T(1,128)}) custom-call(bf16[2304,512]{1,0:T(8,128)(2,1)} %reduce.1.sum_ref, f32[1,1]{1,0:T(1,128)} %get-tuple-element.17.loss_ref), custom_call_target="tpu_custom_call" | custom-call | tf_op jit(solution)/shard_map/tail/pallas_call | solution.py:629

commit v3 on v2

--- a/solution.py
+++ b/solution.py
@@ -65,8 +65,8 @@
 
     pl.semaphore_wait(barrier, 1 + has_right.astype(jnp.int32) + has_left.astype(jnp.int32))
 
-    def rows_of(chip, core):
-        return pl.ds(aligned((chip * 2 + core) * rows, rows), rows)
+    def rows_of(chip):
+        return pl.ds(aligned(chip * 2 * rows, 2 * rows), 2 * rows)
 
     def spot(chip, q):
         return all_ref.at[pl.ds(aligned((chip * 2 + c) * rows + q * piece, piece), piece)]
@@ -82,33 +82,26 @@
         src = pooled_ref.at[pl.ds(q * piece, piece)] if k == 0 else dst
         return remote(src, dst, pair_send.at[k, q], pair_recv.at[k, q], pair)
 
-    def stores(chip, core):
-        span = rows_of(chip, core)
-        which = chip * 2 + core
+    def stores(chip):
+        span = rows_of(chip)
         return [
-            pltpu.make_async_copy(source.at[span], target.at[span], store_sem.at[i, which])
+            pltpu.make_async_copy(source.at[span], target.at[span], store_sem.at[i, chip])
             for i, (source, target) in enumerate(
                 ((all_ref, all_out), (preact_ref, preact_out), (hidden_ref, hidden_out))
             )
         ]
 
-    def head(chip, core, own=False):
-        span = rows_of(chip, core)
-        features = pooled_ref[...] if own else all_ref[span, :]
-        if own:
-            all_ref[span, :] = features
-        preact = jnp.dot(features, first_ref[...], preferred_element_type=F32)
+    def head(k, chip):
+        for q in range(parts):
+            pair_copy(k, chip, q).wait_recv()
+        span = rows_of(chip)
+        preact = jnp.dot(all_ref[span, :], first_ref[...], preferred_element_type=F32)
         preact_ref[span, :] = preact
         hidden = jax.nn.gelu(preact).astype(BF16)
         hidden_ref[span, :] = hidden
         partial_ref[span, :] = jnp.dot(hidden, second_ref[...], preferred_element_type=F32)
-        for copy in stores(chip, core):
+        for copy in stores(chip):
             copy.start()
-
-    def pair_head(k, chip):
-        for q in range(parts):
-            pair_copy(k, chip, q).wait_recv()
-        head(chip, 1 - c)
 
     for q in range(parts):
         for way in range(2):
@@ -118,8 +111,8 @@
                 line_copy(way, 0, q).start()
 
         pair_copy(0, z, q).start()
+    all_ref[pl.ds(aligned(g * rows, rows), rows), :] = pooled_ref[...]
     load.wait()
-    head(z, c, own=True)
 
     def key_of(way, s):
         return 1 + s if way == 0 else n + s
@@ -141,25 +134,19 @@
                     pair_copy(key_of(way, s), chip(s + 1), q).start()
 
         if s == 0:
-            pair_head(0, z)
-        for way in range(2):
-            _, _, chip, arrives = ways[way]
-            if s:
-
-                @pl.when(arrives(s - 1))
+            head(0, z)
+        else:
+            for way in range(2):
+
+                @pl.when(ways[way][3](s - 1))
                 def _():
-                    pair_head(key_of(way, s - 1), chip(s))
-
-            @pl.when(arrives(s))
-            def _():
-                head(chip(s + 1), c)
+                    head(key_of(way, s - 1), ways[way][2](s))
 
     for way in range(2):
-        _, exists, chip, arrives = ways[way]
-
-        @pl.when(arrives(n - 2))
+
+        @pl.when(ways[way][3](n - 2))
         def _():
-            pair_head(key_of(way, n - 2), chip(n - 1))
+            head(key_of(way, n - 2), ways[way][2](n - 1))
 
     for q in range(parts):
         pair_copy(0, z, q).wait_send()
@@ -182,19 +169,21 @@
                             line_copy(way, s + 1, q).wait_send()
 
     for chip in range(n):
-        for core in range(2):
-            for copy in stores(chip, core):
-                copy.wait()
+        for copy in stores(chip):
+            copy.wait()
 
 
 def middle_kernel(
-    cycle, n, part_ref, pos_ref, grad_ref, loss_ref,
+    cycle, n, part_ref, pos_ref, preact_hbm, grad_ref, loss_ref, slope_out,
+    preact_ref, move_sem,
     pbuf, acc, zbuf, unit_ref, length_ref, keys, stats, escore,
     psend, precv, zsend, zrecv, ksend, krecv, ssend, srecv, gsend, grecv,
 ):
     group = 2 * n
     count = cycle * group
     rows, width = unit_ref.shape
+    load = pltpu.make_async_copy(preact_hbm, preact_ref, move_sem.at[0])
+    load.start()
     b = lax.axis_index("blk")
     g = lax.axis_index("grp")
     z, c = g // 2, g % 2
@@ -245,6 +234,18 @@
                     {"grp": ((z + d) % n) * 2 + c},
                 )
             )
+    load.wait()
+
+    def slope(i, carry):
+        span = pl.ds(aligned(i * rows, rows), rows)
+        values = preact_ref[span, :]
+        unused, backward = jax.vjp(jax.nn.gelu, values)
+        preact_ref[span, :] = backward(jnp.ones_like(values))[0]
+        return carry
+
+    lax.fori_loop(0, group, slope, 0)
+    store = pltpu.make_async_copy(preact_ref, slope_out, move_sem.at[1])
+    store.start()
     raw = acc[0]
     for d in range(1, n):
         sums[d].wait_recv()
@@ -390,17 +391,18 @@
         copy.wait_recv()
     for copy in started:
         copy.wait_send()
+    store.wait()
 
 
 def reduce_kernel(
-    cycle, lane_count, grad_ref, second_ref, pooled_hbm, preact_hbm, hidden_hbm, out_ref,
-    pooled_ref, preact_ref, hidden_ref, back_ref, second_grad, acc, sendb, recvb,
+    cycle, lane_count, grad_ref, second_ref, pooled_hbm, slope_hbm, hidden_hbm, out_ref,
+    pooled_ref, slope_ref, hidden_ref, back_ref, second_grad, acc, sendb, recvb,
     load_sem, rs_send, rs_recv, ag_send, ag_recv,
 ):
     loads = [
         pltpu.make_async_copy(source, target, load_sem.at[i])
         for i, (source, target) in enumerate(
-            ((preact_hbm, preact_ref), (hidden_hbm, hidden_ref), (pooled_hbm, pooled_ref))
+            ((slope_hbm, slope_ref), (hidden_hbm, hidden_ref), (pooled_hbm, pooled_ref))
         )
     ]
     for load in loads:
@@ -410,7 +412,7 @@
     bits = [(b // (1 << t)) % 2 for t in range(stages)]
     peers = [{"blk": b + (1 - 2 * bits[t]) * (1 << t)} for t in range(stages)]
     greet(peers)
-    clips = preact_ref.shape[0]
+    clips = slope_ref.shape[0]
     edge = second_ref.shape[1]
     fold = second_ref.shape[0] // edge
     total = out_ref.shape[0]
@@ -427,8 +429,7 @@
             grad_ref[span, :], second_ref[...], (((1,), (1,)), ((), ())),
             preferred_element_type=F32,
         )
-        unused, backward = jax.vjp(jax.nn.gelu, preact_ref[span, :])
-        back_ref[span, :] = backward(hidden_grad)[0].astype(BF16)
+        back_ref[span, :] = (hidden_grad * slope_ref[span, :]).astype(BF16)
         return carry
 
     lax.fori_loop(0, clips // step, back, 0)
@@ -439,18 +440,22 @@
     )
     loads[2].wait()
 
-    def produce(lane):
-        wide = top * cycle
+    def produce(lane, away):
+        t = orders[lane][0]
+        side = (1 - bits[t]) if away else bits[t]
+        units = cycle // 2
+        wide = top * units
+        column = aligned(lane * top * cycle + side * wide, 128)
         first = lax.dot_general(
-            pooled_ref[:, lane * wide : (lane + 1) * wide], back_ref[...], across,
+            pooled_ref[:, pl.ds(column, wide)], back_ref[...], across,
             preferred_element_type=F32,
         )
-        for j in range(cycle):
-            at = lane * size + j * unit
+        for j in range(units):
+            at = aligned(lane * size + (side * units + j) * unit, 16)
             acc[pl.ds(at, top), :] = first[j * top : (j + 1) * top]
-            for t in range(fold):
-                row = t * edge + (lane * cycle + j) * low
-                acc[pl.ds(at + top, low), t * edge : (t + 1) * edge] = second_grad[
+            for k in range(fold):
+                row = aligned(k * edge + (lane * cycle + side * units + j) * low, 16)
+                acc[pl.ds(at + top, low), k * edge : (k + 1) * edge] = second_grad[
                     pl.ds(row, low), :
                 ]
 
@@ -494,8 +499,10 @@
         finals[lane, i] = copy
 
     for lane in range(lane_count):
-        produce(lane)
+        produce(lane, True)
         start_reduce(lane, 0)
+    for lane in range(lane_count):
+        produce(lane, False)
     for i in range(stages):
         for lane in range(lane_count):
             copies[lane, i].wait_recv()
@@ -571,20 +578,23 @@
             pltpu.VMEM((group * rows, units), F32),
             pltpu.VMEM((group * rows, units), BF16),
             DMA((2, n, 2)), DMA((2, n, 2)), DMA((2 * n, 2)), DMA((2 * n, 2)),
-            DMA, DMA((3, group)),
+            DMA, DMA((3, n)),
         ],
         compiler_params=params(0),
         name="head",
     )(pooled, w_first, w_second)
-    group_grad, loss = pl.pallas_call(
+    group_grad, loss, slope = pl.pallas_call(
         functools.partial(middle_kernel, cycle, n),
         out_shape=(
             jax.ShapeDtypeStruct((group * rows, edge), BF16),
             jax.ShapeDtypeStruct((1, 1), F32),
+            jax.ShapeDtypeStruct((group * rows, units), F32),
         ),
-        in_specs=[VMEM] * 2,
-        out_specs=(VMEM, SMEM),
+        in_specs=[VMEM, VMEM, ANY],
+        out_specs=(VMEM, SMEM, ANY),
         scratch_shapes=[
+            pltpu.VMEM((group * rows, units), F32),
+            DMA((2,)),
             pltpu.VMEM((n, rows, edge), F32),
             pltpu.VMEM((n, rows, edge), F32),
             pltpu.VMEM((n, rows, edge), F32),
@@ -599,7 +609,7 @@
         ],
         compiler_params=params(1),
         name="middle",
-    )(partial, positives[None, :])
+    )(partial, positives[None, :], preact)
     fold = units // edge
     total = width + units // fold
     lane_count = 4 if units // fold % (4 * cycle * 16) == 0 else 2
@@ -623,7 +633,7 @@
         ],
         compiler_params=params(2),
         name="reduce",
-    )(group_grad, w_second, pooled_all, preact, hidden)
+    )(group_grad, w_second, pooled_all, slope, hidden)
     unit = total // (lane_count * cycle)
     tiles = lane_count * cycle // 2
     first_out, second_out, loss = pl.pallas_call(

time: 161 us -> 160 us (level)
  no operation moved by 1% of the time
where the time goes in v3:
time: 160 us
  Pallas kernels  153 us (96%)
  matrix products  3.42 us (2%)
  other arithmetic  2.54 us (2%)
    pallas_call x1, Pallas kernels, shards(): pl.pallas_call(functools.partial(middle_kernel, cycle, n), out_shape=(jax...  53.7 us
    pallas_call x1, Pallas kernels, shards(): pl.pallas_call(functools.partial(reduce_kernel, cycle, lane_count), out_s...  48.4 us
    pallas_call x1, Pallas kernels, shards(): pl.pallas_call(functools.partial(head_kernel, n), out_shape=(jax.ShapeDty...  44.1 us
    pallas_call x1, Pallas kernels, shards(): pl.pallas_call(functools.partial(tail_kernel, unit, fold), grid=(tiles,),...  6.82 us
    dot_general x1, matrix products, shards(): jnp.einsum('rf,rfc->rc', frame_mask, frames, preferred_element_type=F32)  3.42 us

profile of v3, /device:TPU:0, one launch (start us, length us, event | category | flops | bytes accessed | tf_op | source)
XLA Modules:
  0.0 159.7 jit_solution(3896731024777450602)
XLA Ops:
  0.6 0.7 convert_element_type.8
  1.3 0.7 fusion.3
  2.0 3.4 %fusion.1 = f32[128,1,2048]{2,1,0:T(1,128)S(1)} fusion(bf16[128,8,2048]{2,1,0:T(8,128)(2,1)} %param.5, pred[128,8,1]{1,0,2:T(32,128)(4,1)S(1)} %fusion.3), kind=kOutput, calls=%fused_computation.2 | convolution fusion | flops 4194304 | bytes 5243904 | tf_op jit(solution)/shard_map/rf,rfc->rc/dot_general | solution.py:563
  5.5 1.1 fusion.pooled_ref
  6.6 44.1 %head.1 = (bf16[1024,2048]{1,0:T(8,128)(2,1)}, f32[1024,512]{1,0:T(8,128)}, bf16[1024,512]{1,0:T(8,128)(2,1)}, f32[1024,256]{1,0:T(8,128)}) custom-call(bf16[128,2048]{1,0:T(8,128)(2,1)} %fusion.pooled_ref, bf16[2048,512]{1,0:T(8,128)(2,1)} %first_hbm.1, bf16[512,256]{1,0:T(8,128)(2,1)} %second_ref.3), custom_call_target="tpu_custom_call" | custom-call | tf_op jit(solution)/shard_map/head/pallas_call | solution.py:565
  50.8 53.7 %middle.1 = (bf16[1024,256]{1,0:T(8,128)(2,1)}, f32[1,1]{1,0:T(1,128)}, f32[1024,512]{1,0:T(8,128)}) custom-call(f32[1024,256]{1,0:T(8,128)} %get-tuple-element.13.part_ref, s32[1,128]{1,0:T(1,128)} %bitcast.10, f32[1024,512]{1,0:T(8,128)} %get-tuple-element.14.preact_hbm), custom_call_target="tpu_custom_call" | custom-call | tf_op jit(solution)/shard_map/middle/pallas_call | solution.py:586
  104.5 48.4 %reduce.1.sum_ref = bf16[2304,512]{1,0:T(8,128)(2,1)} custom-call(bf16[1024,256]{1,0:T(8,128)(2,1)} %get-tuple-element.15.grad_ref, bf16[512,256]{1,0:T(8,128)(2,1)} %second_ref.3, bf16[1024,2048]{1,0:T(8,128)(2,1)} %get-tuple-element.16.pooled_hbm, f32[1024,512]{1,0:T(8,128)} %get-tuple-element.17.slope_hbm, bf16[1024,512]{1,0:T(8,128)(2,1)} %get-tuple-element.18.hidden_hbm), custom_call_target="tpu_custom_call" | custom-call | tf_op jit(solution)/shard_map/reduce/pallas_call | solution.py:618
  152.9 6.8 %tail.1 = (f32[2048,512]{1,0:T(8,128)}, f32[2,256,256]{2,1,0:T(8,128)}, f32[1,1]{1,0:T(1,128)}) custom-call(bf16[2304,512]{1,0:T(8,128)(2,1)} %reduce.1.sum_ref, f32[1,1]{1,0:T(1,128)} %get-tuple-element.19.loss_ref), custom_call_target="tpu_custom_call" | custom-call | tf_op jit(solution)/shard_map/tail/pallas_call | solution.py:639

commit v4 on v3

--- a/solution.py
+++ b/solution.py
@@ -16,13 +16,6 @@
 
 def aligned(start, step):
     return pl.multiple_of(start, step)
-
-
-def greet(partners):
-    barrier = pltpu.get_barrier_semaphore()
-    for device in partners:
-        pl.semaphore_signal(barrier, inc=1, device_id=device, device_id_type=MESH)
-    pl.semaphore_wait(barrier, len(partners))
 
 
 def remote(src, dst, send_sem, recv_sem, device):
@@ -36,10 +29,9 @@
     )
 
 
-def head_kernel(
-    n, pooled_ref, first_hbm, second_ref, all_out, preact_out, hidden_out, partial_ref,
-    first_ref, all_ref, preact_ref, hidden_ref,
-    line_send, line_recv, pair_send, pair_recv, load_sem, store_sem,
+def head_phase(
+    n, pooled_ref, second_ref, partial_ref, first_ref, all_ref, preact_ref, hidden_ref, load,
+    line_send, line_recv, pair_send, pair_recv,
 ):
     rows = pooled_ref.shape[0]
     parts = line_send.shape[2]
@@ -52,19 +44,6 @@
         ({"grp": g + 2}, has_right, lambda s: z - s, lambda s: z - 1 - s >= 0),
         ({"grp": g - 2}, has_left, lambda s: z + s, lambda s: z + 1 + s < n),
     )
-    load = pltpu.make_async_copy(first_hbm, first_ref, load_sem)
-    load.start()
-
-    barrier = pltpu.get_barrier_semaphore()
-    pl.semaphore_signal(barrier, inc=1, device_id=pair, device_id_type=MESH)
-    for device, exists, _, _ in ways:
-
-        @pl.when(exists)
-        def _():
-            pl.semaphore_signal(barrier, inc=1, device_id=device, device_id_type=MESH)
-
-    pl.semaphore_wait(barrier, 1 + has_right.astype(jnp.int32) + has_left.astype(jnp.int32))
-
     def rows_of(chip):
         return pl.ds(aligned(chip * 2 * rows, 2 * rows), 2 * rows)
 
@@ -81,15 +60,6 @@
         dst = spot(chip, q)
         src = pooled_ref.at[pl.ds(q * piece, piece)] if k == 0 else dst
         return remote(src, dst, pair_send.at[k, q], pair_recv.at[k, q], pair)
-
-    def stores(chip):
-        span = rows_of(chip)
-        return [
-            pltpu.make_async_copy(source.at[span], target.at[span], store_sem.at[i, chip])
-            for i, (source, target) in enumerate(
-                ((all_ref, all_out), (preact_ref, preact_out), (hidden_ref, hidden_out))
-            )
-        ]
 
     def head(k, chip):
         for q in range(parts):
@@ -100,8 +70,6 @@
         hidden = jax.nn.gelu(preact).astype(BF16)
         hidden_ref[span, :] = hidden
         partial_ref[span, :] = jnp.dot(hidden, second_ref[...], preferred_element_type=F32)
-        for copy in stores(chip):
-            copy.start()
 
     for q in range(parts):
         for way in range(2):
@@ -168,22 +136,15 @@
                         def _():
                             line_copy(way, s + 1, q).wait_send()
 
-    for chip in range(n):
-        for copy in stores(chip):
-            copy.wait()
-
-
-def middle_kernel(
-    cycle, n, part_ref, pos_ref, preact_hbm, grad_ref, loss_ref, slope_out,
-    preact_ref, move_sem,
+
+def middle_phase(
+    cycle, n, part_ref, pos_ref, grad_ref, loss_ref, preact_ref,
     pbuf, acc, zbuf, unit_ref, length_ref, keys, stats, escore,
     psend, precv, zsend, zrecv, ksend, krecv, ssend, srecv, gsend, grecv,
 ):
     group = 2 * n
     count = cycle * group
     rows, width = unit_ref.shape
-    load = pltpu.make_async_copy(preact_hbm, preact_ref, move_sem.at[0])
-    load.start()
     b = lax.axis_index("blk")
     g = lax.axis_index("grp")
     z, c = g // 2, g % 2
@@ -193,15 +154,6 @@
     def other(k):
         device = (me + k) % count
         return {"blk": device // group, "grp": device % group}
-
-    barrier = pltpu.get_barrier_semaphore()
-
-    def hello(k, carry):
-        pl.semaphore_signal(barrier, inc=1, device_id=other(k), device_id_type=MESH)
-        return carry
-
-    lax.fori_loop(1, count, hello, 0)
-    pl.semaphore_wait(barrier, count - 1)
 
     started = []
 
@@ -234,8 +186,6 @@
                     {"grp": ((z + d) % n) * 2 + c},
                 )
             )
-    load.wait()
-
     def slope(i, carry):
         span = pl.ds(aligned(i * rows, rows), rows)
         values = preact_ref[span, :]
@@ -244,8 +194,6 @@
         return carry
 
     lax.fori_loop(0, group, slope, 0)
-    store = pltpu.make_async_copy(preact_ref, slope_out, move_sem.at[1])
-    store.start()
     raw = acc[0]
     for d in range(1, n):
         sums[d].wait_recv()
@@ -391,27 +339,17 @@
         copy.wait_recv()
     for copy in started:
         copy.wait_send()
-    store.wait()
-
-
-def reduce_kernel(
-    cycle, lane_count, grad_ref, second_ref, pooled_hbm, slope_hbm, hidden_hbm, out_ref,
-    pooled_ref, slope_ref, hidden_ref, back_ref, second_grad, acc, sendb, recvb,
-    load_sem, rs_send, rs_recv, ag_send, ag_recv,
+
+
+def reduce_phase(
+    cycle, lane_count, grad_ref, second_ref, pooled_ref, slope_ref, hidden_ref, out_ref,
+    back_ref, second_grad, acc, sendb, recvb,
+    rs_send, rs_recv, ag_send, ag_recv,
 ):
-    loads = [
-        pltpu.make_async_copy(source, target, load_sem.at[i])
-        for i, (source, target) in enumerate(
-            ((slope_hbm, slope_ref), (hidden_hbm, hidden_ref), (pooled_hbm, pooled_ref))
-        )
-    ]
-    for load in loads:
-        load.start()
     b = lax.axis_index("blk")
     stages = cycle.bit_length() - 1
     bits = [(b // (1 << t)) % 2 for t in range(stages)]
     peers = [{"blk": b + (1 - 2 * bits[t]) * (1 << t)} for t in range(stages)]
-    greet(peers)
     clips = slope_ref.shape[0]
     edge = second_ref.shape[1]
     fold = second_ref.shape[0] // edge
@@ -420,7 +358,6 @@
     unit = size // cycle
     top = pooled_ref.shape[1] // (lane_count * cycle)
     low = unit - top
-    loads[0].wait()
     step = 128
 
     def back(i, carry):
@@ -433,12 +370,10 @@
         return carry
 
     lax.fori_loop(0, clips // step, back, 0)
-    loads[1].wait()
     across = (((0,), (0,)), ((), ()))
     second_grad[...] = lax.dot_general(
         hidden_ref[...], grad_ref[...], across, preferred_element_type=F32
     )
-    loads[2].wait()
 
     def produce(lane, away):
         t = orders[lane][0]
@@ -524,6 +459,38 @@
         copy.wait_send()
 
 
+def step_kernel(
+    cycle, n, lane_count, pooled_ref, first_hbm, second_ref, pos_ref, out_ref, loss_ref,
+    first_ref, all_ref, preact_ref, hidden_ref, partial_ref, grad_ref, load_sem, *rest,
+):
+    group = 2 * n
+    count = cycle * group
+    me = lax.axis_index("blk") * group + lax.axis_index("grp")
+    load = pltpu.make_async_copy(first_hbm, first_ref, load_sem)
+    load.start()
+    barrier = pltpu.get_barrier_semaphore()
+
+    def hello(k, carry):
+        device = (me + k) % count
+        pl.semaphore_signal(
+            barrier, inc=1, device_id={"blk": device // group, "grp": device % group},
+            device_id_type=MESH,
+        )
+        return carry
+
+    lax.fori_loop(1, count, hello, 0)
+    pl.semaphore_wait(barrier, count - 1)
+    head_phase(
+        n, pooled_ref, second_ref, partial_ref, first_ref, all_ref, preact_ref, hidden_ref, load,
+        *rest[:4],
+    )
+    middle_phase(cycle, n, partial_ref, pos_ref, grad_ref, loss_ref, preact_ref, *rest[4:22])
+    reduce_phase(
+        cycle, lane_count, grad_ref, second_ref, all_ref, preact_ref, hidden_ref, out_ref,
+        *rest[22:],
+    )
+
+
 def tail_kernel(unit, fold, sum_ref, loss_ref, first_ref, second_ref, out_ref):
     block = sum_ref[...].astype(F32)
     low = second_ref.shape[1] // (block.shape[0] // unit)
@@ -562,39 +529,28 @@
     frame_mask = (jnp.arange(slot_count, dtype=jnp.int32)[None, :] < counts[:, None]).astype(BF16)
     summed = jnp.einsum("rf,rfc->rc", frame_mask, frames, preferred_element_type=F32)
     pooled = (summed / counts[:, None].astype(F32)).astype(BF16)
-    pooled_all, preact, hidden, partial = pl.pallas_call(
-        functools.partial(head_kernel, n),
+    fold = units // edge
+    total = width + units // fold
+    lane_count = 4 if units // fold % (4 * cycle * 16) == 0 else 2
+    stages = cycle.bit_length() - 1
+    links = (lane_count, stages)
+    summed, loss = pl.pallas_call(
+        functools.partial(step_kernel, cycle, n, lane_count),
         out_shape=(
-            jax.ShapeDtypeStruct((group * rows, width), BF16),
-            jax.ShapeDtypeStruct((group * rows, units), F32),
-            jax.ShapeDtypeStruct((group * rows, units), BF16),
-            jax.ShapeDtypeStruct((group * rows, edge), F32),
+            jax.ShapeDtypeStruct((total, units), BF16),
+            jax.ShapeDtypeStruct((1, 1), F32),
         ),
-        in_specs=[VMEM, ANY, VMEM],
-        out_specs=(ANY, ANY, ANY, VMEM),
+        in_specs=[VMEM, ANY, VMEM, VMEM],
+        out_specs=(VMEM, SMEM),
         scratch_shapes=[
             pltpu.VMEM((width, units), BF16),
             pltpu.VMEM((group * rows, width), BF16),
             pltpu.VMEM((group * rows, units), F32),
             pltpu.VMEM((group * rows, units), BF16),
+            pltpu.VMEM((group * rows, edge), F32),
+            pltpu.VMEM((group * rows, edge), BF16),
+            DMA,
             DMA((2, n, 2)), DMA((2, n, 2)), DMA((2 * n, 2)), DMA((2 * n, 2)),
-            DMA, DMA((3, n)),
-        ],
-        compiler_params=params(0),
-        name="head",
-    )(pooled, w_first, w_second)
-    group_grad, loss, slope = pl.pallas_call(
-        functools.partial(middle_kernel, cycle, n),
-        out_shape=(
-            jax.ShapeDtypeStruct((group * rows, edge), BF16),
-            jax.ShapeDtypeStruct((1, 1), F32),
-            jax.ShapeDtypeStruct((group * rows, units), F32),
-        ),
-        in_specs=[VMEM, VMEM, ANY],
-        out_specs=(VMEM, SMEM, ANY),
-        scratch_shapes=[
-            pltpu.VMEM((group * rows, units), F32),
-            DMA((2,)),
             pltpu.VMEM((n, rows, edge), F32),
             pltpu.VMEM((n, rows, edge), F32),
             pltpu.VMEM((n, rows, edge), F32),
@@ -606,34 +562,16 @@
             DMA((n,)), DMA((n,)), DMA((n,)), DMA((n,)),
             DMA((count,)), DMA((count,)), DMA((count,)), DMA((count,)),
             DMA((2 * n,)), DMA((2 * n,)),
-        ],
-        compiler_params=params(1),
-        name="middle",
-    )(partial, positives[None, :], preact)
-    fold = units // edge
-    total = width + units // fold
-    lane_count = 4 if units // fold % (4 * cycle * 16) == 0 else 2
-    stages = cycle.bit_length() - 1
-    links = (lane_count, stages)
-    summed = pl.pallas_call(
-        functools.partial(reduce_kernel, cycle, lane_count),
-        out_shape=jax.ShapeDtypeStruct((total, units), BF16),
-        in_specs=[VMEM, VMEM, ANY, ANY, ANY],
-        out_specs=VMEM,
-        scratch_shapes=[
-            pltpu.VMEM((group * rows, width), BF16),
-            pltpu.VMEM((group * rows, units), F32),
-            pltpu.VMEM((group * rows, units), BF16),
             pltpu.VMEM((group * rows, units), BF16),
             pltpu.VMEM((units, edge), F32),
             pltpu.VMEM((total, units), F32),
             pltpu.VMEM((total, units), BF16),
             pltpu.VMEM((total, units), BF16),
-            DMA((3,)), DMA(links), DMA(links), DMA(links), DMA(links),
+            DMA(links), DMA(links), DMA(links), DMA(links),
         ],
-        compiler_params=params(2),
-        name="reduce",
-    )(group_grad, w_second, pooled_all, slope, hidden)
+        compiler_params=params(0),
+        name="step",
+    )(pooled, w_first, w_second, positives[None, :])
     unit = total // (lane_count * cycle)
     tiles = lane_count * cycle // 2
     first_out, second_out, loss = pl.pallas_call(

time: 160 us -> 149 us (0.931)
  Pallas kernels: 153 us -> 142 us
    pallas_call x3 -> x1, Pallas kernels: 146 us -> 136 us  [shards(): pl.pallas_call(functools.partial(step_kernel, cycle, n, lane_count), out_...]
where the time goes in v4:
time: 149 us
  Pallas kernels  142 us (95%)
  matrix products  3.42 us (2%)
  other arithmetic  2.54 us (2%)
    pallas_call x1, Pallas kernels, shards(): pl.pallas_call(functools.partial(step_kernel, cycle, n, lane_count), out_...  136 us
    pallas_call x1, Pallas kernels, shards(): pl.pallas_call(functools.partial(tail_kernel, unit, fold), grid=(tiles,),...  6.83 us
    dot_general x1, matrix products, shards(): jnp.einsum('rf,rfc->rc', frame_mask, frames, preferred_element_type=F32)  3.42 us

profile of v4, /device:TPU:0, one launch (start us, length us, event | category | flops | bytes accessed | tf_op | source)
XLA Modules:
  0.0 149.0 jit_solution(12941200418878516605)
XLA Ops:
  0.6 0.7 convert_element_type.8
  1.3 0.7 fusion.3
  2.0 3.4 %fusion.1 = f32[128,1,2048]{2,1,0:T(1,128)S(1)} fusion(bf16[128,8,2048]{2,1,0:T(8,128)(2,1)} %param.5, pred[128,8,1]{1,0,2:T(32,128)(4,1)S(1)} %fusion.3), kind=kOutput, calls=%fused_computation.2 | convolution fusion | flops 4194304 | bytes 5243904 | tf_op jit(solution)/shard_map/rf,rfc->rc/dot_general | solution.py:530
  5.5 1.1 fusion.pooled_ref
  6.6 135.5 %step.1 = (bf16[2304,512]{1,0:T(8,128)(2,1)}, f32[1,1]{1,0:T(1,128)}) custom-call(bf16[128,2048]{1,0:T(8,128)(2,1)} %fusion.pooled_ref, bf16[2048,512]{1,0:T(8,128)(2,1)} %first_hbm.1, bf16[512,256]{1,0:T(8,128)(2,1)} %second_ref.1, s32[1,128]{1,0:T(1,128)} %bitcast.10), custom_call_target="tpu_custom_call" | custom-call | tf_op jit(solution)/shard_map/step/pallas_call | solution.py:537
  142.2 6.8 %tail.1 = (f32[2048,512]{1,0:T(8,128)}, f32[2,256,256]{2,1,0:T(8,128)}, f32[1,1]{1,0:T(1,128)}) custom-call(bf16[2304,512]{1,0:T(8,128)(2,1)} %get-tuple-element.8.sum_ref, f32[1,1]{1,0:T(1,128)} %get-tuple-element.9.loss_ref), custom_call_target="tpu_custom_call" | custom-call | tf_op jit(solution)/shard_map/tail/pallas_call | solution.py:577
